TPU v7x, 128 devices: a whole 4x4x4 slice. The times are simulated.
128 devices in a mesh: row: 8 (over y_lo, z), col: 16 (over x, y_hi, core).
Axes of the slice: x: 4, y: 4 (y_hi: 2, y_lo: 2; y = y_hi * 2 + y_lo), z: 4, core: 2. Of those that a mesh axis runs over, the one named last changes fastest.
Arguments:
- frames: float32 [512, 128, 2048], P(('row', 'col')), may hold values from -1 to 6
- class_index: int32 [128, 2048], P('row', 'col'), may hold values from 0 to 7
- surface_mask: int32 [128, 2048], P('row', 'col'), may hold values 0 or 1
- effusivity: float32 [8], replicated, may hold values from 0.5 to 2
- conductivity: float32 [8], replicated, may hold values from 0.2 to 1
Outputs:
- heat_flux: float32 [128, 2048, 512], P('row', 'col')
All inputs are finite; a program needn't handle non-finite values. No bound on the sum of `surface_mask` on one device may be relied on, other than what follows from the above.
Results may differ from a plain program's by a relative error of at most 0.0003.
Values sent between devices are 32-bit elements; how exact they have to be, the bound alone decides.
No kernel may reach another device: no remote copies, remote signals or barrier semaphores. Data moves between devices by JAX's collectives and lax.ppermute only.
A program may use at most 64 MiB of HBM per device.

v0:
```python
import jax
import jax.numpy as jnp
from jax import lax
from jax.sharding import PartitionSpec as P

PASSES = 3


flux_factor = 1.1283791670955126
lateral_rate = 0.24


def extended(block, sides, width):
    for axis, dim in sides:
        count = lax.axis_size(axis)
        forward = [(i, i + 1) for i in range(count - 1)]
        backward = [(target, source) for source, target in forward]
        low = lax.ppermute(
            lax.slice_in_dim(block, block.shape[dim] - width, None, axis=dim), axis, forward
        )
        high = lax.ppermute(lax.slice_in_dim(block, 0, width, axis=dim), axis, backward)
        block = jnp.concatenate([low, block, high], axis=dim)
    return block


def weights(lagged):
    clipped = jnp.maximum(lagged, 0.0)
    return jnp.where(lagged >= 0.0, 1.0 / (jnp.sqrt(clipped) + jnp.sqrt(clipped + 1.0)), 0.0)


def kernel_from(later, earlier):
    lagged = (later[:, None] - earlier[None, :]).astype(jnp.float32)
    return weights(lagged) - weights(lagged - 1.0)


def relax_once(padded, lateral):
    center = padded[1:-1, 1:-1]
    laplace = (
        padded[2:, 1:-1] + padded[:-2, 1:-1] + padded[1:-1, 2:] + padded[1:-1, :-2] - 4.0 * center
    )
    return center + lateral[:, :, None] * laplace


def per_device(frames, class_index, surface_mask, effusivity, conductivity):
    row_count = lax.axis_size("row")
    col_count = lax.axis_size("col")
    local_frames, height, width = frames.shape
    tile_rows = height // row_count
    tile_cols = width // col_count
    total_frames = local_frames * row_count * col_count
    frame_ids = jnp.arange(total_frames, dtype=jnp.int32)
    contract = (((0,), (1,)), ((), ()))
    kernel = kernel_from(frame_ids, frame_ids)
    blocks = frames.reshape(local_frames, row_count, tile_rows, col_count, tile_cols)
    blocks = blocks.transpose(0, 1, 3, 2, 4).reshape(
        local_frames, row_count * col_count, tile_rows, tile_cols
    )
    convolved = lax.dot_general(
        lax.all_to_all(blocks, ("row", "col"), split_axis=1, concat_axis=0, tiled=True)[:, 0],
        kernel,
        contract,
        precision=lax.Precision.HIGHEST,
    )
    classes = jnp.arange(effusivity.shape[0], dtype=jnp.int32)
    matches = (class_index[:, :, None] == classes[None, None, :]).astype(jnp.float32)
    maskf = surface_mask.astype(jnp.float32)
    gain = flux_factor * jnp.sum(matches * effusivity, axis=-1) * maskf
    lateral = lateral_rate * jnp.sum(matches * conductivity, axis=-1) * maskf
    heat_flux = convolved * gain[:, :, None]
    padded = extended(heat_flux, (("row", 0), ("col", 1)), PASSES)
    lateral_wide = extended(lateral, (("row", 0), ("col", 1)), PASSES - 1)
    for pass_index in range(PASSES):
        margin = PASSES - 1 - pass_index
        offset = PASSES - 1 - margin
        lateral_part = lateral_wide[
            offset : offset + tile_rows + 2 * margin, offset : offset + tile_cols + 2 * margin
        ]
        padded = relax_once(padded, lateral_part)
    heat_flux = padded
    return heat_flux


def solution(mesh):
    in_specs = (P(("row", "col"), None, None), P("row", "col"), P("row", "col"), P(), P())
    out_specs = P("row", "col", None)
    return jax.shard_map(
        per_device, mesh=mesh, in_specs=in_specs, out_specs=out_specs, check_vma=False
    )
```

profile of v0, /device:TPU:27, one launch (start us, length us, event | category | flops | bytes accessed | tf_op | source)
XLA Modules:
  0.0 142.1 jit_solution(14230481234940758568)
XLA Ops:
  0.0 3.1 %copy.11 = f32[64,8,16,128]{3,2,1,0:T(8,128)S(1)} copy(f32[64,8,16,128]{3,1,2,0:T(8,128)} %bitcast.20) | data formatting | bytes 8388608
  3.1 3.3 %copy.9 = f32[4,8,16,16,128]{4,2,0,3,1:T(8,128)} copy(f32[4,8,16,16,128]{4,3,2,1,0:T(8,128)S(1)} %bitcast.18) | data formatting | bytes 8388608 | tf_op jit(solution)/shard_map/reshape | solution.py:54
  6.4 11.0 %all-to-all-start = ((f32[4,128,16,128]{3,2,0,1:T(8,128)}), f32[4,128,16,128]{3,2,0,1:T(8,128)}, u32[]{:S(2)}, u32[]{:S(2)}) async-start(f32[4,128,16,128]{3,2,0,1:T(8,128)} %bitcast.17), calls=%async_computation | async-start | bytes 8388608 | tf_op jit(solution)/shard_map/all_to_all | solution.py:59
  17.5 0.1 select_reduce_fusion
  17.6 49.9 %all-to-all-done = f32[4,128,16,128]{3,2,0,1:T(8,128)} async-done(((f32[4,128,16,128]{3,2,0,1:T(8,128)}), f32[4,128,16,128]{3,2,0,1:T(8,128)}, u32[]{:S(2)}, u32[]{:S(2)}) %all-to-all-start) | async-done | bytes 4194336 | tf_op jit(solution)/shard_map/all_to_all | solution.py:59
  67.5 5.2 %copy.10 = f32[512,16,128]{0,2,1:T(8,128)} copy(f32[512,16,128]{2,1,0:T(8,128)} %bitcast.4) | data formatting | bytes 8388608 | tf_op jit(solution)/shard_map/squeeze | solution.py:59
  72.7 12.1 %fusion.9 = f32[512,2048]{0,1:S(1)} fusion(f32[512,2048]{0,1:T(8,128)} %bitcast.21), kind=kOutput, calls=%fused_computation.20 | convolution fusion | flops 6446645248 | bytes 8388608
  84.8 0.4 multiply_bitcast_fusion
  85.2 0.1 fusion.37
  85.3 4.3 %collective-permute-start = (f32[3,128,512]{2,1,0:T(8,128)S(1)}, f32[3,128,512]{2,1,0:T(8,128)S(1)}, u32[]{:S(2)}, u32[]{:S(2)}) collective-permute-start(f32[3,128,512]{2,1,0:T(8,128)S(1)} %get-tuple-element.9), channel_id=1, source_target_pairs={{0,16},{16,32},{32,48},{48,64},{64,80},{80,96},{96,112},{1,17},{17... | collective-permute-start | bytes 2359304 | tf_op jit(solution)/shard_map/ppermute | solution.py:18
  89.6 3.1 %collective-permute-start.1 = (f32[3,128,512]{2,1,0:T(8,128)S(1)}, f32[3,128,512]{2,1,0:T(8,128)S(1)}, u32[]{:S(2)}, u32[]{:S(2)}) collective-permute-start(f32[3,128,512]{2,1,0:T(8,128)S(1)} %get-tuple-element.10), channel_id=1, source_target_pairs={{16,0},{32,16},{48,32},{64,48},{80,64},{96,80},{112,96},{17,1},{33... | collective-permute-start | bytes 2359304 | tf_op jit(solution)/shard_map/ppermute | solution.py:21
  92.7 2.2 %collective-permute-start.4 = (f32[2,128]{1,0:T(2,128)S(1)}, f32[2,128]{1,0:T(2,128)S(1)}, u32[]{:S(2)}, u32[]{:S(2)}) collective-permute-start(f32[2,128]{1,0:T(2,128)S(1)} %get-tuple-element.13), channel_id=1, source_target_pairs={{0,16},{16,32},{32,48},{48,64},{64,80},{80,96},{96,112},{1,17},{17... | collective-permute-start | bytes 3080 | tf_op jit(solution)/shard_map/ppermute | solution.py:18
  94.9 5.2 %collective-permute-start.5 = (f32[2,128]{1,0:T(2,128)S(1)}, f32[2,128]{1,0:T(2,128)S(1)}, u32[]{:S(2)}, u32[]{:S(2)}) collective-permute-start(f32[2,128]{1,0:T(2,128)S(1)} %get-tuple-element.14), channel_id=1, source_target_pairs={{16,0},{32,16},{48,32},{64,48},{80,64},{96,80},{112,96},{17,1},{33... | collective-permute-start | bytes 3080 | tf_op jit(solution)/shard_map/ppermute | solution.py:21
  100.1 6.8 %collective-permute-done.4 = f32[2,128]{1,0:T(2,128)S(1)} collective-permute-done((f32[2,128]{1,0:T(2,128)S(1)}, f32[2,128]{1,0:T(2,128)S(1)}, u32[]{:S(2)}, u32[]{:S(2)}) %collective-permute-start.4) | collective-permute-done | bytes 1056 | tf_op jit(solution)/shard_map/ppermute | solution.py:18
  107.0 2.8 %collective-permute-done.5 = f32[2,128]{1,0:T(2,128)S(1)} collective-permute-done((f32[2,128]{1,0:T(2,128)S(1)}, f32[2,128]{1,0:T(2,128)S(1)}, u32[]{:S(2)}, u32[]{:S(2)}) %collective-permute-start.5) | collective-permute-done | bytes 1056 | tf_op jit(solution)/shard_map/ppermute | solution.py:21
  109.9 6.4 %collective-permute-start.2 = (f32[22,3,512]{2,1,0:T(4,128)S(1)}, f32[22,3,512]{2,1,0:T(4,128)S(1)}, u32[]{:S(2)}, u32[]{:S(2)}) collective-permute-start(f32[22,3,512]{2,1,0:T(4,128)S(1)} %get-tuple-element.7), channel_id=1, source_target_pairs={{0,1},{1,2},{2,3},{3,4},{4,5},{5,6},{6,7},{7,8},{8,9},{9,10},{10,1... | collective-permute-start | bytes 405512 | tf_op jit(solution)/shard_map/ppermute | solution.py:18
  116.3 1.9 %collective-permute-start.3 = (f32[22,3,512]{2,1,0:T(4,128)S(1)}, f32[22,3,512]{2,1,0:T(4,128)S(1)}, u32[]{:S(2)}, u32[]{:S(2)}) collective-permute-start(f32[22,3,512]{2,1,0:T(4,128)S(1)} %get-tuple-element.8), channel_id=1, source_target_pairs={{1,0},{2,1},{3,2},{4,3},{5,4},{6,5},{7,6},{8,7},{9,8},{10,9},{11,1... | collective-permute-start | bytes 405512 | tf_op jit(solution)/shard_map/ppermute | solution.py:21
  118.3 6.0 %collective-permute-start.6 = (f32[20,2]{1,0:T(8,128)S(1)}, f32[20,2]{1,0:T(8,128)S(1)}, u32[]{:S(2)}, u32[]{:S(2)}) collective-permute-start(f32[20,2]{1,0:T(8,128)S(1)} %get-tuple-element.11), channel_id=1, source_target_pairs={{0,1},{1,2},{2,3},{3,4},{4,5},{5,6},{6,7},{7,8},{8,9},{9,10},{10,1... | collective-permute-start | bytes 488 | tf_op jit(solution)/shard_map/ppermute | solution.py:18
  124.3 2.1 %collective-permute-start.7 = (f32[20,2]{1,0:T(8,128)S(1)}, f32[20,2]{1,0:T(8,128)S(1)}, u32[]{:S(2)}, u32[]{:S(2)}) collective-permute-start(f32[20,2]{1,0:T(8,128)S(1)} %get-tuple-element.12), channel_id=1, source_target_pairs={{1,0},{2,1},{3,2},{4,3},{5,4},{6,5},{7,6},{8,7},{9,8},{10,9},{11,1... | collective-permute-start | bytes 488 | tf_op jit(solution)/shard_map/ppermute | solution.py:21
  126.4 5.3 %collective-permute-done.7 = f32[20,2]{1,0:T(8,128)S(1)} collective-permute-done((f32[20,2]{1,0:T(8,128)S(1)}, f32[20,2]{1,0:T(8,128)S(1)}, u32[]{:S(2)}, u32[]{:S(2)}) %collective-permute-start.7) | collective-permute-done | bytes 192 | tf_op jit(solution)/shard_map/ppermute | solution.py:21
  131.9 1.1 pad_maximum_fusion
  133.0 2.8 %fusion.2 = f32[20,132,512]{2,1,0:T(8,128)S(1)} fusion(f32[22,134,512]{2,1,0:T(8,128)S(1)} %pad_maximum_fusion, f32[20,132]{1,0:T(8,128)S(1)} %pad_maximum_fusion.4), kind=kLoop, calls=%fused_computation.4 | loop fusion | flops 9461760 | bytes 32450880 | tf_op jit(solution)/shard_map/add | solution.py:41
  135.8 2.8 %fusion.5 = f32[18,130,512]{2,1,0:T(8,128)S(1)} fusion(f32[20,132,512]{2,1,0:T(8,128)S(1)} %fusion.2, f32[18,130]{1,0:T(8,128)S(1)} %slice.108), kind=kLoop, calls=%fused_computation.10 | loop fusion | flops 8386560 | bytes 28763280 | tf_op jit(solution)/shard_map/add | solution.py:41
  138.6 3.4 %fusion.8 = f32[16,128,512]{2,1,0:T(8,128)} fusion(f32[18,130,512]{2,1,0:T(8,128)S(1)} %fusion.5, f32[16,128]{1,0:T(8,128)S(1)} %get-tuple-element.15), kind=kLoop, calls=%fused_computation.16 | loop fusion | flops 7340032 | bytes 25174016 | tf_op jit(solution)/shard_map/add | solution.py:41
  (20 shorter events, 0.4 us)
Async XLA Ops:
  6.4 11.1 %copy-start = (s32[16,128]{1,0:T(8,128)S(1)}, s32[16,128]{1,0:T(8,128)}, u32[]{:S(2)}) copy-start(s32[16,128]{1,0:T(8,128)} %param.6) | copy-start | bytes 24580
  6.4 11.1 %copy-start.2 = (f32[8]{0:T(128)S(1)}, f32[8]{0:T(128)}, u32[]{:S(2)}) copy-start(f32[8]{0:T(128)} %param.9) | copy-start | bytes 100
  6.4 11.1 %copy-start.3 = (f32[8]{0:T(128)S(1)}, f32[8]{0:T(128)}, u32[]{:S(2)}) copy-start(f32[8]{0:T(128)} %param.8) | copy-start | bytes 100
  6.4 11.2 %copy-start.1 = (s32[16,128]{1,0:T(8,128)S(1)}, s32[16,128]{1,0:T(8,128)}, u32[]{:S(2)}) copy-start(s32[16,128]{1,0:T(8,128)} %param.7) | copy-start | bytes 24580
  6.4 61.1 %all-to-all-start = ((f32[4,128,16,128]{3,2,0,1:T(8,128)}), f32[4,128,16,128]{3,2,0,1:T(8,128)}, u32[]{:S(2)}, u32[]{:S(2)}) async-start(f32[4,128,16,128]{3,2,0,1:T(8,128)} %bitcast.17), calls=%async_computation | async-start | bytes 8388608 | tf_op jit(solution)/shard_map/all_to_all | solution.py:59
  85.3 24.5 %collective-permute-start = (f32[3,128,512]{2,1,0:T(8,128)S(1)}, f32[3,128,512]{2,1,0:T(8,128)S(1)}, u32[]{:S(2)}, u32[]{:S(2)}) collective-permute-start(f32[3,128,512]{2,1,0:T(8,128)S(1)} %get-tuple-element.9), channel_id=1, source_target_pairs={{0,16},{16,32},{32,48},{48,64},{64,80},{80,96},{96,112},{1,17},{17... | collective-permute-start | bytes 2359304 | tf_op jit(solution)/shard_map/ppermute | solution.py:18
  89.6 20.2 %collective-permute-start.1 = (f32[3,128,512]{2,1,0:T(8,128)S(1)}, f32[3,128,512]{2,1,0:T(8,128)S(1)}, u32[]{:S(2)}, u32[]{:S(2)}) collective-permute-start(f32[3,128,512]{2,1,0:T(8,128)S(1)} %get-tuple-element.10), channel_id=1, source_target_pairs={{16,0},{32,16},{48,32},{64,48},{80,64},{96,80},{112,96},{17,1},{33... | collective-permute-start | bytes 2359304 | tf_op jit(solution)/shard_map/ppermute | solution.py:21
  92.7 14.2 %collective-permute-start.4 = (f32[2,128]{1,0:T(2,128)S(1)}, f32[2,128]{1,0:T(2,128)S(1)}, u32[]{:S(2)}, u32[]{:S(2)}) collective-permute-start(f32[2,128]{1,0:T(2,128)S(1)} %get-tuple-element.13), channel_id=1, source_target_pairs={{0,16},{16,32},{32,48},{48,64},{64,80},{80,96},{96,112},{1,17},{17... | collective-permute-start | bytes 3080 | tf_op jit(solution)/shard_map/ppermute | solution.py:18
  94.9 14.9 %collective-permute-start.5 = (f32[2,128]{1,0:T(2,128)S(1)}, f32[2,128]{1,0:T(2,128)S(1)}, u32[]{:S(2)}, u32[]{:S(2)}) collective-permute-start(f32[2,128]{1,0:T(2,128)S(1)} %get-tuple-element.14), channel_id=1, source_target_pairs={{16,0},{32,16},{48,32},{64,48},{80,64},{96,80},{112,96},{17,1},{33... | collective-permute-start | bytes 3080 | tf_op jit(solution)/shard_map/ppermute | solution.py:21
  109.9 22.0 %collective-permute-start.2 = (f32[22,3,512]{2,1,0:T(4,128)S(1)}, f32[22,3,512]{2,1,0:T(4,128)S(1)}, u32[]{:S(2)}, u32[]{:S(2)}) collective-permute-start(f32[22,3,512]{2,1,0:T(4,128)S(1)} %get-tuple-element.7), channel_id=1, source_target_pairs={{0,1},{1,2},{2,3},{3,4},{4,5},{5,6},{6,7},{7,8},{8,9},{9,10},{10,1... | collective-permute-start | bytes 405512 | tf_op jit(solution)/shard_map/ppermute | solution.py:18
  116.3 15.6 %collective-permute-start.3 = (f32[22,3,512]{2,1,0:T(4,128)S(1)}, f32[22,3,512]{2,1,0:T(4,128)S(1)}, u32[]{:S(2)}, u32[]{:S(2)}) collective-permute-start(f32[22,3,512]{2,1,0:T(4,128)S(1)} %get-tuple-element.8), channel_id=1, source_target_pairs={{1,0},{2,1},{3,2},{4,3},{5,4},{6,5},{7,6},{8,7},{9,8},{10,9},{11,1... | collective-permute-start | bytes 405512 | tf_op jit(solution)/shard_map/ppermute | solution.py:21
  118.3 8.2 %collective-permute-start.6 = (f32[20,2]{1,0:T(8,128)S(1)}, f32[20,2]{1,0:T(8,128)S(1)}, u32[]{:S(2)}, u32[]{:S(2)}) collective-permute-start(f32[20,2]{1,0:T(8,128)S(1)} %get-tuple-element.11), channel_id=1, source_target_pairs={{0,1},{1,2},{2,3},{3,4},{4,5},{5,6},{6,7},{7,8},{8,9},{9,10},{10,1... | collective-permute-start | bytes 488 | tf_op jit(solution)/shard_map/ppermute | solution.py:18
  124.3 7.4 %collective-permute-start.7 = (f32[20,2]{1,0:T(8,128)S(1)}, f32[20,2]{1,0:T(8,128)S(1)}, u32[]{:S(2)}, u32[]{:S(2)}) collective-permute-start(f32[20,2]{1,0:T(8,128)S(1)} %get-tuple-element.12), channel_id=1, source_target_pairs={{1,0},{2,1},{3,2},{4,3},{5,4},{6,5},{7,6},{8,7},{9,8},{10,9},{11,1... | collective-permute-start | bytes 488 | tf_op jit(solution)/shard_map/ppermute | solution.py:21
where the time goes:
time: 143 us; the launch traced here: 142 us
  waiting for transfers between devices  64.9 us (45%)
  starting transfers between devices  42.2 us (30%)
  matrix products  12.1 us (8%)
  local copies, waits for them, and re-layouts  11.9 us (8%)
  other arithmetic  10.7 us (7%)
    all_to_all x1, waiting for transfers between devices, per_device(): lax.all_to_all(blocks, ('row', 'col'), split_axis=1, concat_axis=0, tiled...  49.9 us
    ppermute x4, starting transfers between devices, extended(): lax.ppermute(lax.slice_in_dim(block, block.shape[dim] - width, None, axis...  18.9 us
    ppermute x4, starting transfers between devices, extended(): lax.ppermute(lax.slice_in_dim(block, 0, width, axis=dim), axis, backward)  12.3 us
    unnamed x1, matrix products  12.1 us
    all_to_all x1, starting transfers between devices, per_device(): lax.all_to_all(blocks, ('row', 'col'), split_axis=1, concat_axis=0, tiled...  11 us
    add x3, other arithmetic, relax_once(): return center + lateral[:, :, None] * laplace  9.04 us
    ppermute x4, waiting for transfers between devices, extended(): lax.ppermute(lax.slice_in_dim(block, 0, width, axis=dim), axis, backward)  8.15 us
    ppermute x4, waiting for transfers between devices, extended(): lax.ppermute(lax.slice_in_dim(block, block.shape[dim] - width, None, axis...  6.84 us
  transfers between devices with their start and end apart: 9, of which 4 were waited for; matrix products, arithmetic and copies ran while one was open for 0% of the time, Pallas kernels for 0%

commit v1 on v0

v1 whole, which is shorter than its diff:
```python
import functools

import jax
import jax.numpy as jnp
from jax import lax
from jax.experimental import pallas as pl
from jax.experimental.pallas import tpu as pltpu
from jax.sharding import Mesh
from jax.sharding import PartitionSpec as P

PASSES = 3
LANES = 128
SUB = 8

flux_factor = 1.1283791670955126
lateral_rate = 0.24

ALL = ("row", "chip", "core")


def weights(lagged):
    clipped = jnp.maximum(lagged, 0.0)
    return jnp.where(lagged >= 0.0, 1.0 / (jnp.sqrt(clipped) + jnp.sqrt(clipped + 1.0)), 0.0)


def kernel_from(later, earlier):
    lagged = (later[:, None] - earlier[None, :]).astype(jnp.float32)
    return weights(lagged) - weights(lagged - 1.0)


def smooth_body(tiles_down, tile_rows, chips, core_ref, frame_ref, mine_ref, other_ref, out_ref, gain, lat, own, ping, pong):
    tiles_across = 2 * chips
    rows = tiles_down * tile_rows
    core = core_ref[0]

    @pl.when(pl.program_id(0) == 0)
    def _():
        for tile in range(tiles_down):
            for chip in range(chips):
                part = tile * chips + chip
                at = pl.ds(tile * tile_rows, tile_rows)
                for ref, index in ((mine_ref, 2 * chip + core), (other_ref, 2 * chip + 1 - core)):
                    gain[index, at, :] = ref[part, 0:tile_rows, :]
                    lateral = ref[part, tile_rows : 2 * tile_rows, :]
                    lat[index, at, :] = lateral
                    own[index, at, :] = 1.0 - 4.0 * lateral
        edge = jnp.zeros((tiles_across, SUB, LANES), jnp.float32)
        for buffer in (ping, pong):
            buffer[:, 0:SUB, :] = edge
            buffer[:, SUB + rows : 2 * SUB + rows, :] = edge

    lane = lax.broadcasted_iota(jnp.int32, (SUB, LANES), 1)
    first, last = lane == 0, lane == LANES - 1

    @pl.loop(0, rows // SUB)
    def _(i):
        at = pl.ds(pl.multiple_of(i * SUB, SUB), SUB)
        for c in range(tiles_across):
            ping[c, pl.ds(pl.multiple_of(i * SUB + SUB, SUB), SUB), :] = (
                frame_ref[0, at, c * LANES : (c + 1) * LANES] * gain[c, at, :]
            )

    def one_pass(source, store):
        @pl.loop(0, rows // SUB)
        def _(i):
            at = pl.ds(pl.multiple_of(i * SUB, SUB), SUB)
            zero = jnp.zeros((SUB, LANES), jnp.float32)
            center = [source[c, pl.ds(pl.multiple_of(i * SUB + SUB, SUB), SUB), :] for c in range(tiles_across)]
            right_moved = [pltpu.roll(v, 1, 1) for v in center]
            left_moved = [pltpu.roll(v, LANES - 1, 1) for v in center]
            for c in range(tiles_across):
                up = source[c, pl.ds(i * SUB + SUB - 1, SUB), :]
                down = source[c, pl.ds(i * SUB + SUB + 1, SUB), :]
                left = jnp.where(first, right_moved[c - 1] if c > 0 else zero, right_moved[c])
                right = jnp.where(last, left_moved[c + 1] if c + 1 < tiles_across else zero, left_moved[c])
                around = (up + down) + (left + right)
                store(i, c, own[c, at, :] * center[c] + lat[c, at, :] * around)

    def into(buffer):
        def store(i, c, value):
            buffer[c, pl.ds(pl.multiple_of(i * SUB + SUB, SUB), SUB), :] = value

        return store

    def deliver(i, c, value):
        steps = tile_rows // SUB
        at = pl.ds(pl.multiple_of((i % steps) * SUB, SUB), SUB)
        out_ref[(i // steps) * tiles_across + c, at, :] = value

    buffers = (ping, pong)
    for index in range(PASSES):
        target = deliver if index == PASSES - 1 else into(buffers[(index + 1) % 2])
        one_pass(buffers[index % 2], target)


def smooth(core, frames, mine, other, tiles_down, tile_rows, chips):
    count, height, width = frames.shape
    across = 2 * chips
    devices = tiles_down * across
    whole = lambda f, core: (0, 0, 0)
    return pl.pallas_call(
        functools.partial(smooth_body, tiles_down, tile_rows, chips),
        out_shape=jax.ShapeDtypeStruct((devices, count * tile_rows, LANES), jnp.float32),
        grid_spec=pltpu.PrefetchScalarGridSpec(
            num_scalar_prefetch=1,
            grid=(count,),
            in_specs=[
                pl.BlockSpec((1, height, width), lambda f, core: (f, 0, 0)),
                pl.BlockSpec(mine.shape, whole),
                pl.BlockSpec(other.shape, whole),
            ],
            out_specs=pl.BlockSpec((devices, tile_rows, LANES), lambda f, core: (0, f, 0)),
            scratch_shapes=[pltpu.VMEM((across, height, LANES), jnp.float32)] * 3
            + [pltpu.VMEM((across, height + 2 * SUB, LANES), jnp.float32)] * 2,
        ),
        compiler_params=pltpu.CompilerParams(vmem_limit_bytes=48 << 20),
        name="smooth",
    )(core, frames, mine, other)


def convolve_body(count, tile_rows, devices, x_ref, high_ref, low_ref, out_ref):
    for r in range(tile_rows):
        parts = [x_ref[pl.ds(f * tile_rows + r, devices, stride=count * tile_rows), :] for f in range(count)]
        x = jnp.concatenate(parts, axis=0).T
        high = x.astype(jnp.bfloat16)
        low = (x - high.astype(jnp.float32)).astype(jnp.bfloat16)
        dot = lambda a, b: jnp.dot(a, b, preferred_element_type=jnp.float32)
        out_ref[r] = dot(high, high_ref[...]) + (dot(high, low_ref[...]) + dot(low, high_ref[...]))


def convolve(blocks, high, low, count, tile_rows):
    devices = blocks.shape[0]
    return pl.pallas_call(
        functools.partial(convolve_body, count, tile_rows, devices),
        out_shape=jax.ShapeDtypeStruct((tile_rows, LANES, high.shape[1]), jnp.float32),
        compiler_params=pltpu.CompilerParams(vmem_limit_bytes=48 << 20),
        name="convolve",
    )(blocks.reshape(devices * count * tile_rows, LANES), high, low)


def per_device(frames, class_index, surface_mask, effusivity, conductivity):
    tiles_down, chips = lax.axis_size("row"), lax.axis_size("chip")
    tile_rows = class_index.shape[0]
    count = frames.shape[0]
    devices = tiles_down * chips * 2
    core = lax.axis_index("core")

    classes = jnp.arange(effusivity.shape[0], dtype=jnp.int32)
    matches = (class_index[:, :, None] == classes[None, None, :]).astype(jnp.float32)
    maskf = surface_mask.astype(jnp.float32)
    gain = flux_factor * jnp.sum(matches * effusivity, axis=-1) * maskf
    lateral = lateral_rate * jnp.sum(matches * conductivity, axis=-1) * maskf
    maps = jnp.concatenate([gain, lateral], axis=0)
    peers = tiles_down * chips
    mine = lax.all_to_all(
        jnp.broadcast_to(maps[None], (peers, 2 * tile_rows, LANES)), ("row", "chip"), split_axis=0, concat_axis=0, tiled=True
    )
    other = lax.ppermute(mine, "core", [(0, 1), (1, 0)])
    blocks = smooth(core[None].astype(jnp.int32), frames, mine, other, tiles_down, tile_rows, chips)

    frame_ids = jnp.arange(devices * count, dtype=jnp.int32)
    arrival = frame_ids % devices * count + frame_ids // devices
    kernel = kernel_from(frame_ids, arrival).T
    rounded = lax.reduce_precision(kernel, 8, 7)
    high, low = rounded.astype(jnp.bfloat16), (kernel - rounded).astype(jnp.bfloat16)

    received = lax.all_to_all(blocks, ALL, split_axis=0, concat_axis=0, tiled=True)
    return convolve(received, high, low, count, tile_rows)


def solution(mesh):
    cores = Mesh(mesh.devices.reshape(mesh.shape["row"], mesh.shape["col"] // 2, 2), ALL)
    tile = P("row", ("chip", "core"))
    in_specs = (P(ALL, None, None), tile, tile, P(), P())
    return jax.shard_map(
        per_device, mesh=cores, in_specs=in_specs, out_specs=P("row", ("chip", "core"), None), check_vma=False
    )
```

time: 143 us -> 127 us (0.89)
  the two profiles are of different devices: /device:TPU:27 before, /device:TPU:4 now
where the time goes in v1:
time: 127 us; the launch traced here: 126 us
  waiting for transfers between devices  54.7 us (43%)
  Pallas kernels  33.4 us (26%)
  blocking collectives  27.7 us (22%)
  starting transfers between devices  7.02 us (6%)
  other arithmetic  3.44 us (3%)
    all_to_all x1, waiting for transfers between devices, per_device(): lax.all_to_all(blocks, ALL, split_axis=0, concat_axis=0, tiled=True)  52 us
    all_to_all x1, blocking collectives, per_device(): lax.all_to_all(jnp.broadcast_to(maps[None], (peers, 2 * tile_rows, LANES)...  27.7 us
    pallas_call x1, Pallas kernels, smooth(): pl.pallas_call(functools.partial(smooth_body, tiles_down, tile_rows, chip...  24.1 us
    pallas_call x1, Pallas kernels, convolve(): pl.pallas_call(functools.partial(convolve_body, count, tile_rows, devices...  9.34 us
    all_to_all x1, starting transfers between devices, per_device(): lax.all_to_all(blocks, ALL, split_axis=0, concat_axis=0, tiled=True)  7.02 us
    ppermute x1, waiting for transfers between devices, per_device(): other = lax.ppermute(mine, 'core', [(0, 1), (1, 0)])  2.66 us
  transfers between devices with their start and end apart: 2, of which 2 were waited for; matrix products, arithmetic and copies ran while one was open for 2% of the time, Pallas kernels for 0%

profile of v1, /device:TPU:4, one launch (start us, length us, event | category | flops | bytes accessed | tf_op | source)
XLA Modules:
  0.0 126.4 jit_solution(3349231210891014349)
XLA Ops:
  0.0 0.8 select_reduce_fusion.1
  0.8 0.7 convert_multiply_fusion
  1.5 0.1 broadcast_in_dim.7
  1.6 27.7 %all_to_all.10.mine_ref = f32[64,32,128]{2,1,0:T(8,128)S(1)} all-to-all(f32[64,32,128]{2,1,0:T(8,128)S(1)} %broadcast_in_dim.7), channel_id=1, replica_groups=mesh['row'=8,'chip'=8,'core'=2] {'row','chip'}, dimensions={0} | all-to-all | bytes 2097152 | tf_op jit(solution)/shard_map/all_to_all | solution.py:155
  29.3 0.0 collective-permute-start
  29.3 2.7 %collective-permute-done.other_ref = f32[64,32,128]{2,1,0:T(8,128)S(1)} collective-permute-done((f32[64,32,128]{2,1,0:T(8,128)S(1)}, f32[64,32,128]{2,1,0:T(8,128)S(1)}, u32[]{:S(2)}, u32[]{:S(2)}) %collective-permute-start) | collective-permute-done | bytes 1048608 | tf_op jit(solution)/shard_map/ppermute | solution.py:158
  32.0 24.1 %smooth.1 = f32[128,64,128]{2,1,0:T(8,128)} custom-call(s32[1]{0:T(128)} %bitcast.core_ref, f32[4,128,2048]{2,1,0:T(8,128)} %frame_ref.1, f32[64,32,128]{2,1,0:T(8,128)S(1)} %all_to_all.10.mine_ref, f32[64,32,128]{2,1,0:T(8,128)S(1)} %collective-permute-done.other_ref), custom_call_target="tpu_custom_call" | custom-call | tf_op jit(solution)/shard_map/smooth/pallas_call | solution.py:101
  56.1 7.0 %all-to-all-start.1 = ((f32[128,64,128]{2,1,0:T(8,128)}), f32[128,64,128]{2,1,0:T(8,128)}, u32[]{:S(2)}, u32[]{:S(2)}) async-start(f32[128,64,128]{2,1,0:T(8,128)} %smooth.1), calls=%async_computation.1 | async-start | bytes 8388608 | tf_op jit(solution)/shard_map/all_to_all | solution.py:167
  63.1 1.9 %fusion = (bf16[512,512]{1,0:T(8,128)(2,1)S(1)}, bf16[512,512]{1,0:T(8,128)(2,1)S(1)}) fusion(s32[512]{0:T(512)S(1)} %fusion.6), kind=kLoop, calls=%fused_computation.2 | loop fusion | flops 5242880 | bytes 1050624 | tf_op jit(solution)/shard_map/convert_element_type | solution.py:165
  65.0 52.0 %all-to-all-done.1 = f32[128,64,128]{2,1,0:T(8,128)} async-done(((f32[128,64,128]{2,1,0:T(8,128)}), f32[128,64,128]{2,1,0:T(8,128)}, u32[]{:S(2)}, u32[]{:S(2)}) %all-to-all-start.1) | async-done | bytes 4194336 | tf_op jit(solution)/shard_map/all_to_all | solution.py:167
  117.0 9.3 %convolve.1 = f32[16,128,512]{2,1,0:T(8,128)} custom-call(f32[8192,128]{1,0:T(8,128)} %bitcast.1.x_ref, bf16[512,512]{1,0:T(8,128)(2,1)S(1)} %get-tuple-element.10.high_ref, bf16[512,512]{1,0:T(8,128)(2,1)S(1)} %get-tuple-element.9.low_ref), custom_call_target="tpu_custom_call" | custom-call | tf_op jit(solution)/shard_map/convolve/pallas_call | solution.py:133
  (2 shorter events, 0.0 us)
Async XLA Ops:
  29.3 2.7 %collective-permute-start = (f32[64,32,128]{2,1,0:T(8,128)S(1)}, f32[64,32,128]{2,1,0:T(8,128)S(1)}, u32[]{:S(2)}, u32[]{:S(2)}) collective-permute-start(f32[64,32,128]{2,1,0:T(8,128)S(1)} %all_to_all.10.mine_ref), channel_id=1, source_target_pairs={{0,1},{1,0},{2,3},{3,2},{4,5},{5,4},{6,7},{7,6},{8,9},{9,8},{10,11... | collective-permute-start | bytes 3145736 | tf_op jit(solution)/shard_map/ppermute | solution.py:158
  56.1 61.0 %all-to-all-start.1 = ((f32[128,64,128]{2,1,0:T(8,128)}), f32[128,64,128]{2,1,0:T(8,128)}, u32[]{:S(2)}, u32[]{:S(2)}) async-start(f32[128,64,128]{2,1,0:T(8,128)} %smooth.1), calls=%async_computation.1 | async-start | bytes 8388608 | tf_op jit(solution)/shard_map/all_to_all | solution.py:167

commit v2 on v1

v2 whole, which is shorter than its diff:
```python
import functools

import jax
import jax.numpy as jnp
from jax import lax
from jax.experimental import pallas as pl
from jax.experimental.pallas import tpu as pltpu
from jax.sharding import Mesh
from jax.sharding import PartitionSpec as P

PASSES = 3
LANES = 128
SUB = 8

flux_factor = 1.1283791670955126
lateral_rate = 0.24

ALL = ("row", "chip", "core")


def weights(lagged):
    clipped = jnp.maximum(lagged, 0.0)
    return jnp.where(lagged >= 0.0, 1.0 / (jnp.sqrt(clipped) + jnp.sqrt(clipped + 1.0)), 0.0)


def kernel_from(later, earlier):
    lagged = (later[:, None] - earlier[None, :]).astype(jnp.float32)
    return weights(lagged) - weights(lagged - 1.0)


def smooth_body(
    tiles_down, tile_rows, chips,
    core_ref, frames_ref, mine_ref, other_ref, out_ref,
    loaded, gain, lat, own, ping, pong, ready, load_sem, store_sem,
):
    tiles_across = 2 * chips
    count, rows, _ = frames_ref.shape
    core = core_ref[0]
    steps = rows // SUB

    def load(f):
        return pltpu.make_async_copy(frames_ref.at[f], loaded.at[f], load_sem.at[f])

    def deliver(slot, f):
        part = pl.ds(pl.multiple_of(f * tile_rows, tile_rows), tile_rows)
        return pltpu.make_async_copy(ready.at[slot], out_ref.at[:, part, :], store_sem.at[slot])

    for f in range(count):
        load(f).start()
    for tile in range(tiles_down):
        for chip in range(chips):
            part = tile * chips + chip
            at = pl.ds(tile * tile_rows, tile_rows)
            for ref, index in ((mine_ref, 2 * chip + core), (other_ref, 2 * chip + 1 - core)):
                gain[index, at, :] = ref[part, 0:tile_rows, :]
                lateral = ref[part, tile_rows : 2 * tile_rows, :]
                lat[index, at, :] = lateral
                own[index, at, :] = 1.0 - 4.0 * lateral
    zero = jnp.zeros((SUB, LANES), jnp.float32)
    for buffer in (ping, pong):
        for c in range(tiles_across):
            buffer[c, 0:SUB, :] = zero
            buffer[c, SUB + rows : 2 * SUB + rows, :] = zero

    lane = lax.broadcasted_iota(jnp.int32, (SUB, LANES), 1)
    first, last = lane == 0, lane == LANES - 1

    def one_pass(source, store):
        for half in range(0, steps, SUB):
            center, right_moved, left_moved = {}, {}, {}

            def prepare(c):
                for i in range(half, half + SUB):
                    value = source[c, SUB + i * SUB : 2 * SUB + i * SUB, :]
                    center[c, i] = value
                    right_moved[c, i] = pltpu.roll(value, 1, 1)
                    left_moved[c, i] = pltpu.roll(value, LANES - 1, 1)

            prepare(0)
            for c in range(tiles_across):
                if c + 1 < tiles_across:
                    prepare(c + 1)
                for i in range(half, half + SUB):
                    at = slice(i * SUB, i * SUB + SUB)
                    up = source[c, SUB - 1 + i * SUB : 2 * SUB - 1 + i * SUB, :]
                    down = source[c, SUB + 1 + i * SUB : 2 * SUB + 1 + i * SUB, :]
                    left = jnp.where(first, right_moved[c - 1, i] if c > 0 else zero, right_moved[c, i])
                    right = jnp.where(last, left_moved[c + 1, i] if c + 1 < tiles_across else zero, left_moved[c, i])
                    around = (up + down) + (left + right)
                    store(i, c, own[c, at, :] * center[c, i] + lat[c, at, :] * around)

    def into(buffer):
        def store(i, c, value):
            buffer[c, SUB + i * SUB : 2 * SUB + i * SUB, :] = value

        return store

    buffers = (ping, pong)

    @pl.loop(0, count)
    def _(f):
        slot = f % 2
        load(f).wait()

        @pl.when(f >= 2)
        def _():
            deliver(slot, f - 2).wait()

        for c in range(tiles_across):
            ping[c, SUB : SUB + rows, :] = loaded[f, :, c * LANES : (c + 1) * LANES] * gain[c]

        def finish(i, c, value):
            tile, part = i * SUB // tile_rows, i * SUB % tile_rows
            ready[slot, tile * tiles_across + c, part : part + SUB, :] = value

        for index in range(PASSES):
            one_pass(buffers[index % 2], finish if index == PASSES - 1 else into(buffers[(index + 1) % 2]))
        deliver(slot, f).start()

    for f in range(count - 2, count):
        deliver(f % 2, f).wait()


def smooth(core, frames, mine, other, tiles_down, tile_rows, chips):
    count, height, width = frames.shape
    across = 2 * chips
    devices = tiles_down * across
    return pl.pallas_call(
        functools.partial(smooth_body, tiles_down, tile_rows, chips),
        out_shape=jax.ShapeDtypeStruct((devices, count * tile_rows, LANES), jnp.float32),
        in_specs=[pl.BlockSpec(memory_space=pltpu.SMEM), pl.BlockSpec(memory_space=pltpu.HBM)]
        + [pl.BlockSpec(memory_space=pltpu.VMEM)] * 2,
        out_specs=pl.BlockSpec(memory_space=pltpu.HBM),
        scratch_shapes=[pltpu.VMEM((count, height, width), jnp.float32)]
        + [pltpu.VMEM((across, height, LANES), jnp.float32)] * 3
        + [pltpu.VMEM((across, height + 2 * SUB, LANES), jnp.float32)] * 2
        + [pltpu.VMEM((2, devices, tile_rows, LANES), jnp.float32)]
        + [pltpu.SemaphoreType.DMA((count,)), pltpu.SemaphoreType.DMA((2,))],
        compiler_params=pltpu.CompilerParams(vmem_limit_bytes=56 << 20),
        name="smooth",
    )(core, frames, mine, other)


def convolve_body(count, devices, x_ref, high_ref, low_ref, out_ref):
    rows, _, outputs = out_ref.shape
    flat = x_ref.reshape(devices * count * SUB, LANES)
    base = pl.program_id(0) * rows % SUB
    early = devices // 2
    high, low = [], []
    for r in range(rows):
        pieces = []
        for start in (0, early):
            for pair in range(0, count, 2):
                both = [
                    flat[pl.ds((start * count + f) * SUB + base + r, early, stride=count * SUB), :]
                    for f in (pair, pair + 1)
                ]
                pieces.append(jnp.concatenate(both, axis=0).T)
        x = jnp.concatenate(pieces, axis=1)
        top = x.astype(jnp.bfloat16)
        high.append(top)
        low.append((x - top.astype(jnp.float32)).astype(jnp.bfloat16))
    high, low = jnp.concatenate(high, axis=0), jnp.concatenate(low, axis=0)

    def product(depth, columns):
        def dot(a, b_ref):
            return jnp.dot(a[:, :depth], b_ref[:depth, columns], preferred_element_type=jnp.float32)

        result = dot(high, high_ref) + (dot(high, low_ref) + dot(low, high_ref))
        out_ref[:, :, columns] = result.reshape(rows, LANES, -1)

    half = outputs // 2
    product(half, slice(0, half))
    product(outputs, slice(half, outputs))


def convolve(blocks, high, low, count, tile_rows):
    devices = blocks.shape[0]
    frames = high.shape[1]
    step = SUB // 2
    return pl.pallas_call(
        functools.partial(convolve_body, count, devices),
        out_shape=jax.ShapeDtypeStruct((tile_rows, LANES, frames), jnp.float32),
        grid=(tile_rows // step,),
        in_specs=[
            pl.BlockSpec((devices, count, 1, SUB, LANES), lambda i: (0, 0, i * step // SUB, 0, 0)),
            pl.BlockSpec((frames, frames), lambda i: (0, 0)),
            pl.BlockSpec((frames, frames), lambda i: (0, 0)),
        ],
        out_specs=pl.BlockSpec((step, LANES, frames), lambda i: (i, 0, 0)),
        compiler_params=pltpu.CompilerParams(vmem_limit_bytes=24 << 20),
        name="convolve",
    )(blocks.reshape(devices, count, tile_rows // SUB, SUB, LANES), high, low)


def per_device(frames, class_index, surface_mask, effusivity, conductivity):
    tiles_down, chips = lax.axis_size("row"), lax.axis_size("chip")
    tile_rows = class_index.shape[0]
    count = frames.shape[0]
    devices = tiles_down * chips * 2
    core = lax.axis_index("core")

    classes = jnp.arange(effusivity.shape[0], dtype=jnp.int32)
    matches = (class_index[:, :, None] == classes[None, None, :]).astype(jnp.float32)
    maskf = surface_mask.astype(jnp.float32)
    gain = flux_factor * jnp.sum(matches * effusivity, axis=-1) * maskf
    lateral = lateral_rate * jnp.sum(matches * conductivity, axis=-1) * maskf
    maps = jnp.concatenate([gain, lateral], axis=0)
    peers = tiles_down * chips
    mine = lax.all_to_all(
        jnp.broadcast_to(maps[None], (peers, 2 * tile_rows, LANES)), ("row", "chip"), split_axis=0, concat_axis=0, tiled=True
    )
    other = lax.ppermute(mine, "core", [(0, 1), (1, 0)])
    blocks = smooth(core[None].astype(jnp.int32), frames, mine, other, tiles_down, tile_rows, chips)

    frame_ids = jnp.arange(devices * count, dtype=jnp.int32)
    early = devices // 2
    source = frame_ids // (early * count) * early + frame_ids % early
    arrival = source * count + frame_ids // early % count
    kernel = kernel_from(frame_ids, arrival).T
    rounded = lax.reduce_precision(kernel, 8, 7)
    high, low = rounded.astype(jnp.bfloat16), (kernel - rounded).astype(jnp.bfloat16)

    received = lax.all_to_all(blocks, ALL, split_axis=0, concat_axis=0, tiled=True)
    return convolve(received, high, low, count, tile_rows)


def solution(mesh):
    cores = Mesh(mesh.devices.reshape(mesh.shape["row"], mesh.shape["col"] // 2, 2), ALL)
    tile = P("row", ("chip", "core"))
    in_specs = (P(ALL, None, None), tile, tile, P(), P())
    return jax.shard_map(
        per_device, mesh=cores, in_specs=in_specs, out_specs=P("row", ("chip", "core"), None), check_vma=False
    )
```

time: 127 us -> 113 us (0.89)
  Pallas kernels: 33.4 us -> 19 us
    pallas_call x1, Pallas kernels: 24.1 us -> 10.8 us  [smooth(): pl.pallas_call(functools.partial(smooth_body, tiles_down, tile_rows, chip...]
where the time goes in v2:
time: 113 us
  waiting for transfers between devices  54.7 us (48%)
  blocking collectives  27.7 us (25%)
  Pallas kernels  19 us (17%)
  starting transfers between devices  7.03 us (6%)
  other arithmetic  3.44 us (3%)
  local copies, waits for them, and re-layouts  1.14 us (1%)
    all_to_all x1, waiting for transfers between devices, per_device(): lax.all_to_all(blocks, ALL, split_axis=0, concat_axis=0, tiled=True)  52 us
    all_to_all x1, blocking collectives, per_device(): lax.all_to_all(jnp.broadcast_to(maps[None], (peers, 2 * tile_rows, LANES)...  27.7 us
    pallas_call x1, Pallas kernels, smooth(): pl.pallas_call(functools.partial(smooth_body, tiles_down, tile_rows, chip...  10.8 us
    pallas_call x1, Pallas kernels, convolve(): pl.pallas_call(functools.partial(convolve_body, count, devices), out_shap...  8.19 us
    all_to_all x1, starting transfers between devices, per_device(): lax.all_to_all(blocks, ALL, split_axis=0, concat_axis=0, tiled=True)  7.03 us
    ppermute x1, waiting for transfers between devices, per_device(): other = lax.ppermute(mine, 'core', [(0, 1), (1, 0)])  2.66 us
  transfers between devices with their start and end apart: 2, of which 2 were waited for; matrix products, arithmetic and copies ran while one was open for 2% of the time, Pallas kernels for 0%

profile of v2, /device:TPU:4, one launch (start us, length us, event | category | flops | bytes accessed | tf_op | source)
XLA Modules:
  0.0 113.0 jit_solution(11060680934989914272)
XLA Ops:
  0.0 0.8 select_reduce_fusion.1
  0.8 0.7 convert_multiply_fusion
  1.5 0.1 broadcast_in_dim.7
  1.6 27.7 %all_to_all.10.mine_ref = f32[64,32,128]{2,1,0:T(8,128)S(1)} all-to-all(f32[64,32,128]{2,1,0:T(8,128)S(1)} %broadcast_in_dim.7), channel_id=1, replica_groups=mesh['row'=8,'chip'=8,'core'=2] {'row','chip'}, dimensions={0} | all-to-all | bytes 2097152 | tf_op jit(solution)/shard_map/all_to_all | solution.py:210
  29.3 0.0 copy-start
  29.3 0.0 collective-permute-start
  29.3 2.7 %collective-permute-done.other_ref = f32[64,32,128]{2,1,0:T(8,128)S(1)} collective-permute-done((f32[64,32,128]{2,1,0:T(8,128)S(1)}, f32[64,32,128]{2,1,0:T(8,128)S(1)}, u32[]{:S(2)}, u32[]{:S(2)}) %collective-permute-start) | collective-permute-done | bytes 1048608 | tf_op jit(solution)/shard_map/ppermute | solution.py:213
  32.0 0.0 copy-start.1
  32.0 0.0 copy-done
  32.0 1.0 copy-done.1
  33.0 10.8 %smooth.1 = f32[128,64,128]{2,1,0:T(8,128)} custom-call(s32[1]{0:T(128)} %bitcast.core_ref, f32[4,128,2048]{2,1,0:T(8,128)} %frames_ref.1, f32[64,32,128]{2,1,0:T(8,128)} %copy-done, f32[64,32,128]{2,1,0:T(8,128)} %copy-done.1), custom_call_target="tpu_custom_call" | custom-call | tf_op jit(solution)/shard_map/smooth/pallas_call | solution.py:128
  43.8 7.0 %all-to-all-start.1 = ((f32[128,64,128]{2,1,0:T(8,128)}), f32[128,64,128]{2,1,0:T(8,128)}, u32[]{:S(2)}, u32[]{:S(2)}) async-start(f32[128,64,128]{2,1,0:T(8,128)} %smooth.1), calls=%async_computation.1 | async-start | bytes 8388608 | tf_op jit(solution)/shard_map/all_to_all | solution.py:224
  50.9 1.9 %fusion = (bf16[512,512]{1,0:T(8,128)(2,1)S(1)}, bf16[512,512]{1,0:T(8,128)(2,1)S(1)}) fusion(s32[512]{0:T(512)S(1)} %fusion.9), kind=kLoop, calls=%fused_computation.2 | loop fusion | flops 5242880 | bytes 1050624 | tf_op jit(solution)/shard_map/convert_element_type | solution.py:222
  52.8 52.0 %all-to-all-done.1 = f32[128,64,128]{2,1,0:T(8,128)} async-done(((f32[128,64,128]{2,1,0:T(8,128)}), f32[128,64,128]{2,1,0:T(8,128)}, u32[]{:S(2)}, u32[]{:S(2)}) %all-to-all-start.1) | async-done | bytes 4194336 | tf_op jit(solution)/shard_map/all_to_all | solution.py:224
  104.8 8.2 %convolve.1 = f32[16,128,512]{2,1,0:T(8,128)} custom-call(f32[128,4,2,8,128]{4,3,2,1,0:T(8,128)} %bitcast.1.x_ref, bf16[512,512]{1,0:T(8,128)(2,1)S(1)} %get-tuple-element.10.high_ref, bf16[512,512]{1,0:T(8,128)(2,1)S(1)} %get-tuple-element.9.low_ref), custom_call_target="tpu_custom_call" | custom-call | tf_op jit(solution)/shard_map/convolve/pallas_call | solution.py:181
  (2 shorter events, 0.0 us)
Async XLA Ops:
  29.3 2.7 %copy-start = (f32[64,32,128]{2,1,0:T(8,128)}, f32[64,32,128]{2,1,0:T(8,128)S(1)}, u32[]{:S(2)}) copy-start(f32[64,32,128]{2,1,0:T(8,128)S(1)} %all_to_all.10.mine_ref) | copy-start | bytes 3145732
  29.3 2.7 %collective-permute-start = (f32[64,32,128]{2,1,0:T(8,128)S(1)}, f32[64,32,128]{2,1,0:T(8,128)S(1)}, u32[]{:S(2)}, u32[]{:S(2)}) collective-permute-start(f32[64,32,128]{2,1,0:T(8,128)S(1)} %all_to_all.10.mine_ref), channel_id=1, source_target_pairs={{0,1},{1,0},{2,3},{3,2},{4,5},{5,4},{6,7},{7,6},{8,9},{9,8},{10,11... | collective-permute-start | bytes 3145736 | tf_op jit(solution)/shard_map/ppermute | solution.py:213
  32.0 1.0 copy-start.1
  43.8 61.0 %all-to-all-start.1 = ((f32[128,64,128]{2,1,0:T(8,128)}), f32[128,64,128]{2,1,0:T(8,128)}, u32[]{:S(2)}, u32[]{:S(2)}) async-start(f32[128,64,128]{2,1,0:T(8,128)} %smooth.1), calls=%async_computation.1 | async-start | bytes 8388608 | tf_op jit(solution)/shard_map/all_to_all | solution.py:224

commit v3 on v2

--- a/solution.py
+++ b/solution.py
@@ -11,6 +11,7 @@
 PASSES = 3
 LANES = 128
 SUB = 8
+ROW_GROUP = 2
 
 flux_factor = 1.1283791670955126
 lateral_rate = 0.24
@@ -136,61 +137,110 @@
         + [pltpu.VMEM((across, height + 2 * SUB, LANES), jnp.float32)] * 2
         + [pltpu.VMEM((2, devices, tile_rows, LANES), jnp.float32)]
         + [pltpu.SemaphoreType.DMA((count,)), pltpu.SemaphoreType.DMA((2,))],
-        compiler_params=pltpu.CompilerParams(vmem_limit_bytes=56 << 20),
+        compiler_params=pltpu.CompilerParams(vmem_limit_bytes=50 << 20),
         name="smooth",
     )(core, frames, mine, other)
 
 
-def convolve_body(count, devices, x_ref, high_ref, low_ref, out_ref):
-    rows, _, outputs = out_ref.shape
-    flat = x_ref.reshape(devices * count * SUB, LANES)
-    base = pl.program_id(0) * rows % SUB
-    early = devices // 2
-    high, low = [], []
-    for r in range(rows):
-        pieces = []
-        for start in (0, early):
-            for pair in range(0, count, 2):
-                both = [
-                    flat[pl.ds((start * count + f) * SUB + base + r, early, stride=count * SUB), :]
-                    for f in (pair, pair + 1)
-                ]
-                pieces.append(jnp.concatenate(both, axis=0).T)
-        x = jnp.concatenate(pieces, axis=1)
-        top = x.astype(jnp.bfloat16)
-        high.append(top)
-        low.append((x - top.astype(jnp.float32)).astype(jnp.bfloat16))
-    high, low = jnp.concatenate(high, axis=0), jnp.concatenate(low, axis=0)
-
-    def product(depth, columns):
-        def dot(a, b_ref):
-            return jnp.dot(a[:, :depth], b_ref[:depth, columns], preferred_element_type=jnp.float32)
+def convolve_body(count, rows, x_ref, high_ref, low_ref, out_ref, loaded, high, low, ready, load_sem, early_sem, late_sem):
+    quarters, chunk, _ = loaded.shape
+    sources = chunk // (count * rows)
+    outputs = out_ref.shape[2]
+    half = outputs // 2
+    first, second = slice(0, half), slice(half, outputs)
+    groups = rows // ROW_GROUP
+
+    def load(q):
+        return pltpu.make_async_copy(x_ref.at[pl.ds(q * chunk, chunk)], loaded.at[q], load_sem.at[q])
+
+    def save(k, columns, sem):
+        part = slice(k * ROW_GROUP, (k + 1) * ROW_GROUP)
+        return pltpu.make_async_copy(ready.at[part, :, columns], out_ref.at[part, :, columns], sem.at[k])
+
+    def prepare(q, k):
+        flat = loaded.at[q]
+        for r in range(k * ROW_GROUP, (k + 1) * ROW_GROUP):
+            parts = [flat[pl.ds(f * rows + r, sources, stride=count * rows), :] for f in range(count)]
+            x = jnp.concatenate(parts, axis=0).T
+            top = x.astype(jnp.bfloat16)
+            at = (slice(r * LANES, (r + 1) * LANES), slice(q * LANES, (q + 1) * LANES))
+            high[at] = top
+            low[at] = (x - top.astype(jnp.float32)).astype(jnp.bfloat16)
+
+    def product(k, terms, columns):
+        at = (slice(k * ROW_GROUP * LANES, (k + 1) * ROW_GROUP * LANES), terms)
+
+        def dot(a_ref, b_ref):
+            return jnp.dot(a_ref[at], b_ref[terms, columns], preferred_element_type=jnp.float32)
 
         result = dot(high, high_ref) + (dot(high, low_ref) + dot(low, high_ref))
-        out_ref[:, :, columns] = result.reshape(rows, LANES, -1)
-
-    half = outputs // 2
-    product(half, slice(0, half))
-    product(outputs, slice(half, outputs))
+        return result.reshape(ROW_GROUP, LANES, half)
+
+    for q in range(quarters):
+        load(q).start()
+    load(0).wait()
+    for k in range(groups):
+        prepare(0, k)
+    load(1).wait()
+    for k in range(groups):
+        part = slice(k * ROW_GROUP, (k + 1) * ROW_GROUP)
+        prepare(1, k)
+        ready[part, :, first] = product(k, first, first)
+        save(k, first, early_sem).start()
+        ready[part, :, second] = product(k, first, second)
+    load(2).wait()
+    load(3).wait()
+    for k in range(groups):
+        part = slice(k * ROW_GROUP, (k + 1) * ROW_GROUP)
+        prepare(2, k)
+        prepare(3, k)
+        ready[part, :, second] = ready[part, :, second] + product(k, second, second)
+        save(k, second, late_sem).start()
+    for k in range(groups):
+        save(k, first, early_sem).wait()
+        save(k, second, late_sem).wait()
 
 
 def convolve(blocks, high, low, count, tile_rows):
     devices = blocks.shape[0]
     frames = high.shape[1]
-    step = SUB // 2
+    quarters = 4
     return pl.pallas_call(
-        functools.partial(convolve_body, count, devices),
+        functools.partial(convolve_body, count, tile_rows),
         out_shape=jax.ShapeDtypeStruct((tile_rows, LANES, frames), jnp.float32),
-        grid=(tile_rows // step,),
-        in_specs=[
-            pl.BlockSpec((devices, count, 1, SUB, LANES), lambda i: (0, 0, i * step // SUB, 0, 0)),
-            pl.BlockSpec((frames, frames), lambda i: (0, 0)),
-            pl.BlockSpec((frames, frames), lambda i: (0, 0)),
-        ],
-        out_specs=pl.BlockSpec((step, LANES, frames), lambda i: (i, 0, 0)),
-        compiler_params=pltpu.CompilerParams(vmem_limit_bytes=24 << 20),
+        in_specs=[pl.BlockSpec(memory_space=pltpu.HBM)] + [pl.BlockSpec(memory_space=pltpu.VMEM)] * 2,
+        out_specs=pl.BlockSpec(memory_space=pltpu.HBM),
+        scratch_shapes=[pltpu.VMEM((quarters, devices // quarters * count * tile_rows, LANES), jnp.float32)]
+        + [pltpu.VMEM((tile_rows * LANES, frames), jnp.bfloat16)] * 2
+        + [pltpu.VMEM((tile_rows, LANES, frames), jnp.float32)]
+        + [pltpu.SemaphoreType.DMA((quarters,))]
+        + [pltpu.SemaphoreType.DMA((tile_rows // ROW_GROUP,))] * 2,
+        compiler_params=pltpu.CompilerParams(vmem_limit_bytes=50 << 20),
         name="convolve",
-    )(blocks.reshape(devices, count, tile_rows // SUB, SUB, LANES), high, low)
+    )(blocks.reshape(devices * count * tile_rows, LANES), high, low)
+
+
+def maps_body(class_ref, mask_ref, effusivity_ref, conductivity_ref, out_ref):
+    classes, mask = class_ref[...], mask_ref[...].astype(jnp.float32)
+    rows = classes.shape[0]
+    gain = lateral = jnp.zeros_like(mask)
+    for k in range(effusivity_ref.shape[0]):
+        gain = jnp.where(classes == k, effusivity_ref[k], gain)
+        lateral = jnp.where(classes == k, conductivity_ref[k], lateral)
+    gain, lateral = flux_factor * gain * mask, lateral_rate * lateral * mask
+    out_ref[0:rows, :] = gain
+    out_ref[rows : 2 * rows, :] = lateral
+
+
+def maps_for(class_index, surface_mask, effusivity, conductivity):
+    rows = class_index.shape[0]
+    return pl.pallas_call(
+        maps_body,
+        out_shape=jax.ShapeDtypeStruct((2 * rows, LANES), jnp.float32),
+        in_specs=[pl.BlockSpec(memory_space=pltpu.VMEM)] * 2 + [pl.BlockSpec(memory_space=pltpu.SMEM)] * 2,
+        out_specs=pl.BlockSpec(memory_space=pltpu.VMEM),
+        name="maps",
+    )(class_index, surface_mask, effusivity, conductivity)
 
 
 def per_device(frames, class_index, surface_mask, effusivity, conductivity):
@@ -200,23 +250,16 @@
     devices = tiles_down * chips * 2
     core = lax.axis_index("core")
 
-    classes = jnp.arange(effusivity.shape[0], dtype=jnp.int32)
-    matches = (class_index[:, :, None] == classes[None, None, :]).astype(jnp.float32)
-    maskf = surface_mask.astype(jnp.float32)
-    gain = flux_factor * jnp.sum(matches * effusivity, axis=-1) * maskf
-    lateral = lateral_rate * jnp.sum(matches * conductivity, axis=-1) * maskf
-    maps = jnp.concatenate([gain, lateral], axis=0)
-    peers = tiles_down * chips
-    mine = lax.all_to_all(
-        jnp.broadcast_to(maps[None], (peers, 2 * tile_rows, LANES)), ("row", "chip"), split_axis=0, concat_axis=0, tiled=True
-    )
+    maps = maps_for(class_index, surface_mask, effusivity, conductivity)
+    for_all = jnp.broadcast_to(maps[None], (tiles_down * chips, *maps.shape))
+    mine = lax.all_to_all(for_all, ("row", "chip"), split_axis=0, concat_axis=0, tiled=True)
     other = lax.ppermute(mine, "core", [(0, 1), (1, 0)])
     blocks = smooth(core[None].astype(jnp.int32), frames, mine, other, tiles_down, tile_rows, chips)
 
     frame_ids = jnp.arange(devices * count, dtype=jnp.int32)
-    early = devices // 2
-    source = frame_ids // (early * count) * early + frame_ids % early
-    arrival = source * count + frame_ids // early % count
+    quarter = devices // 4
+    source = frame_ids // (quarter * count) * quarter + frame_ids % quarter
+    arrival = source * count + frame_ids // quarter % count
     kernel = kernel_from(frame_ids, arrival).T
     rounded = lax.reduce_precision(kernel, 8, 7)
     high, low = rounded.astype(jnp.bfloat16), (kernel - rounded).astype(jnp.bfloat16)

time: 113 us -> 110 us (0.973)
  other arithmetic: 3.44 us -> 1.93 us
    pallas_call x1, Pallas kernels: 10.8 us -> 9.24 us  [smooth(): pl.pallas_call(functools.partial(smooth_body, tiles_down, tile_rows, chip...]
    pallas_call x1 -> x2, Pallas kernels: 8.19 us -> 8.68 us  [the longest x1 7.25 us: convolve(): pl.pallas_call(functools.partial(convolve_body, count, tile_rows), out_sh...]
where the time goes in v3:
time: 110 us
  waiting for transfers between devices  54.7 us (50%)
  blocking collectives  27.7 us (25%)
  Pallas kernels  17.9 us (16%)
  starting transfers between devices  7.02 us (6%)
  other arithmetic  1.93 us (2%)
    all_to_all x1, waiting for transfers between devices, per_device(): lax.all_to_all(blocks, ALL, split_axis=0, concat_axis=0, tiled=True)  52 us
    all_to_all x1, blocking collectives, per_device(): lax.all_to_all(for_all, ('row', 'chip'), split_axis=0, concat_axis=0, til...  27.7 us
    pallas_call x1, Pallas kernels, smooth(): pl.pallas_call(functools.partial(smooth_body, tiles_down, tile_rows, chip...  9.24 us
    pallas_call x1, Pallas kernels, convolve(): pl.pallas_call(functools.partial(convolve_body, count, tile_rows), out_sh...  7.25 us
    all_to_all x1, starting transfers between devices, per_device(): lax.all_to_all(blocks, ALL, split_axis=0, concat_axis=0, tiled=True)  7.02 us
    ppermute x1, waiting for transfers between devices, per_device(): other = lax.ppermute(mine, 'core', [(0, 1), (1, 0)])  2.66 us
  transfers between devices with their start and end apart: 2, of which 2 were waited for; matrix products, arithmetic and copies ran while one was open for 2% of the time, Pallas kernels for 0%

profile of v3, /device:TPU:4, one launch (start us, length us, event | category | flops | bytes accessed | tf_op | source)
XLA Modules:
  0.0 110.1 jit_solution(16720945168962174452)
XLA Ops:
  0.0 1.4 %maps.1 = f32[32,128]{1,0:T(8,128)} custom-call(s32[16,128]{1,0:T(8,128)} %class_ref.1, s32[16,128]{1,0:T(8,128)} %mask_ref.1, f32[8]{0:T(128)} %effusivity_ref.1, f32[8]{0:T(128)} %conductivity_ref.1), custom_call_target="tpu_custom_call" | custom-call | tf_op jit(solution)/shard_map/maps/pallas_call | solution.py:237
  1.4 0.8 broadcast_in_dim.7
  2.3 27.7 %all_to_all.10.mine_ref = f32[64,32,128]{2,1,0:T(8,128)S(1)} all-to-all(f32[64,32,128]{2,1,0:T(8,128)S(1)} %broadcast_in_dim.7), channel_id=1, replica_groups=mesh['row'=8,'chip'=8,'core'=2] {'row','chip'}, dimensions={0} | all-to-all | bytes 2097152 | tf_op jit(solution)/shard_map/all_to_all | solution.py:255
  30.0 0.0 collective-permute-start
  30.0 2.7 %collective-permute-done.other_ref = f32[64,32,128]{2,1,0:T(8,128)S(1)} collective-permute-done((f32[64,32,128]{2,1,0:T(8,128)S(1)}, f32[64,32,128]{2,1,0:T(8,128)S(1)}, u32[]{:S(2)}, u32[]{:S(2)}) %collective-permute-start) | collective-permute-done | bytes 1048608 | tf_op jit(solution)/shard_map/ppermute | solution.py:256
  32.6 9.2 %smooth.1 = f32[128,64,128]{2,1,0:T(8,128)} custom-call(s32[1]{0:T(128)} %bitcast.core_ref, f32[4,128,2048]{2,1,0:T(8,128)} %frames_ref.1, f32[64,32,128]{2,1,0:T(8,128)S(1)} %all_to_all.10.mine_ref, f32[64,32,128]{2,1,0:T(8,128)S(1)} %collective-permute-done.other_ref), custom_call_target="tpu_custom_call" | custom-call | tf_op jit(solution)/shard_map/smooth/pallas_call | solution.py:129
  41.9 7.0 %all-to-all-start.1 = ((f32[128,64,128]{2,1,0:T(8,128)}), f32[128,64,128]{2,1,0:T(8,128)}, u32[]{:S(2)}, u32[]{:S(2)}) async-start(f32[128,64,128]{2,1,0:T(8,128)} %smooth.1), calls=%async_computation.1 | async-start | bytes 8388608 | tf_op jit(solution)/shard_map/all_to_all | solution.py:267
  48.9 1.9 %fusion = (bf16[512,512]{1,0:T(8,128)(2,1)S(1)}, bf16[512,512]{1,0:T(8,128)(2,1)S(1)}) fusion(s32[512]{0:T(512)S(1)} %fusion.9), kind=kLoop, calls=%fused_computation.2 | loop fusion | flops 5242880 | bytes 1050624 | tf_op jit(solution)/shard_map/convert_element_type | solution.py:265
  50.8 52.0 %all-to-all-done.1 = f32[128,64,128]{2,1,0:T(8,128)} async-done(((f32[128,64,128]{2,1,0:T(8,128)}), f32[128,64,128]{2,1,0:T(8,128)}, u32[]{:S(2)}, u32[]{:S(2)}) %all-to-all-start.1) | async-done | bytes 4194336 | tf_op jit(solution)/shard_map/all_to_all | solution.py:267
  102.9 7.3 %convolve.1 = f32[16,128,512]{2,1,0:T(8,128)} custom-call(f32[8192,128]{1,0:T(8,128)} %bitcast.1.x_ref, bf16[512,512]{1,0:T(8,128)(2,1)S(1)} %get-tuple-element.6.high_ref, bf16[512,512]{1,0:T(8,128)(2,1)S(1)} %get-tuple-element.5.low_ref), custom_call_target="tpu_custom_call" | custom-call | tf_op jit(solution)/shard_map/convolve/pallas_call | solution.py:208
  (1 shorter events, 0.0 us)
Async XLA Ops:
  30.0 2.7 %collective-permute-start = (f32[64,32,128]{2,1,0:T(8,128)S(1)}, f32[64,32,128]{2,1,0:T(8,128)S(1)}, u32[]{:S(2)}, u32[]{:S(2)}) collective-permute-start(f32[64,32,128]{2,1,0:T(8,128)S(1)} %all_to_all.10.mine_ref), channel_id=1, source_target_pairs={{0,1},{1,0},{2,3},{3,2},{4,5},{5,4},{6,7},{7,6},{8,9},{9,8},{10,11... | collective-permute-start | bytes 3145736 | tf_op jit(solution)/shard_map/ppermute | solution.py:256
  41.9 61.0 %all-to-all-start.1 = ((f32[128,64,128]{2,1,0:T(8,128)}), f32[128,64,128]{2,1,0:T(8,128)}, u32[]{:S(2)}, u32[]{:S(2)}) async-start(f32[128,64,128]{2,1,0:T(8,128)} %smooth.1), calls=%async_computation.1 | async-start | bytes 8388608 | tf_op jit(solution)/shard_map/all_to_all | solution.py:267

commit v4 on v3

--- a/solution.py
+++ b/solution.py
@@ -8,7 +8,6 @@
 from jax.sharding import Mesh
 from jax.sharding import PartitionSpec as P
 
-PASSES = 3
 LANES = 128
 SUB = 8
 ROW_GROUP = 2
@@ -31,7 +30,7 @@
 
 def smooth_body(
     tiles_down, tile_rows, chips,
-    core_ref, frames_ref, mine_ref, other_ref, out_ref,
+    core_ref, table_ref, frames_ref, mine_ref, other_ref, out_ref,
     loaded, gain, lat, own, ping, pong, ready, load_sem, store_sem,
 ):
     tiles_across = 2 * chips
@@ -42,21 +41,28 @@
     def load(f):
         return pltpu.make_async_copy(frames_ref.at[f], loaded.at[f], load_sem.at[f])
 
-    def deliver(slot, f):
+    def deliver(slot, f, half):
         part = pl.ds(pl.multiple_of(f * tile_rows, tile_rows), tile_rows)
-        return pltpu.make_async_copy(ready.at[slot], out_ref.at[:, part, :], store_sem.at[slot])
-
-    for f in range(count):
-        load(f).start()
+        to = pl.ds(half * (tiles_down // 2) * tiles_across, tiles_down // 2 * tiles_across)
+        return pltpu.make_async_copy(ready.at[slot, to], out_ref.at[to, part, :], store_sem.at[slot, half])
+
+    load(0).start()
     for tile in range(tiles_down):
         for chip in range(chips):
             part = tile * chips + chip
             at = pl.ds(tile * tile_rows, tile_rows)
             for ref, index in ((mine_ref, 2 * chip + core), (other_ref, 2 * chip + 1 - core)):
-                gain[index, at, :] = ref[part, 0:tile_rows, :]
-                lateral = ref[part, tile_rows : 2 * tile_rows, :]
+                lateral = ref[part, 0:tile_rows, :]
+                if ref.shape[1] == 2 * tile_rows:
+                    gain[index, at, :] = ref[part, tile_rows : 2 * tile_rows, :]
+                else:
+                    found = jnp.zeros_like(lateral)
+                    for k in range(table_ref.shape[1]):
+                        found = jnp.where(lateral == table_ref[0, k], table_ref[1, k], found)
+                    gain[index, at, :] = found
                 lat[index, at, :] = lateral
                 own[index, at, :] = 1.0 - 4.0 * lateral
+    load(1).start()
     zero = jnp.zeros((SUB, LANES), jnp.float32)
     for buffer in (ping, pong):
         for c in range(tiles_across):
@@ -66,7 +72,7 @@
     lane = lax.broadcasted_iota(jnp.int32, (SUB, LANES), 1)
     first, last = lane == 0, lane == LANES - 1
 
-    def one_pass(source, store):
+    def one_pass(source, store, after=None):
         for half in range(0, steps, SUB):
             center, right_moved, left_moved = {}, {}, {}
 
@@ -89,57 +95,64 @@
                     right = jnp.where(last, left_moved[c + 1, i] if c + 1 < tiles_across else zero, left_moved[c, i])
                     around = (up + down) + (left + right)
                     store(i, c, own[c, at, :] * center[c, i] + lat[c, at, :] * around)
+            if after:
+                after(half // SUB)
 
     def into(buffer):
         def store(i, c, value):
             buffer[c, SUB + i * SUB : 2 * SUB + i * SUB, :] = value
 
         return store
-
-    buffers = (ping, pong)
 
     @pl.loop(0, count)
     def _(f):
         slot = f % 2
         load(f).wait()
 
+        @pl.when(f + 2 < count)
+        def _():
+            load(f + 2).start()
+
+        for c in range(tiles_across):
+            ping[c, SUB : SUB + rows, :] = loaded[f, :, c * LANES : (c + 1) * LANES] * gain[c]
+        one_pass(ping, into(pong))
+        one_pass(pong, into(ping))
+
         @pl.when(f >= 2)
         def _():
-            deliver(slot, f - 2).wait()
-
-        for c in range(tiles_across):
-            ping[c, SUB : SUB + rows, :] = loaded[f, :, c * LANES : (c + 1) * LANES] * gain[c]
+            for half in range(2):
+                deliver(slot, f - 2, half).wait()
 
         def finish(i, c, value):
             tile, part = i * SUB // tile_rows, i * SUB % tile_rows
             ready[slot, tile * tiles_across + c, part : part + SUB, :] = value
 
-        for index in range(PASSES):
-            one_pass(buffers[index % 2], finish if index == PASSES - 1 else into(buffers[(index + 1) % 2]))
-        deliver(slot, f).start()
+        one_pass(ping, finish, lambda half: deliver(slot, f, half).start())
 
     for f in range(count - 2, count):
-        deliver(f % 2, f).wait()
-
-
-def smooth(core, frames, mine, other, tiles_down, tile_rows, chips):
+        for half in range(2):
+            deliver(f % 2, f, half).wait()
+
+
+def smooth(core, table, frames, mine, other, tiles_down, tile_rows, chips):
     count, height, width = frames.shape
     across = 2 * chips
     devices = tiles_down * across
     return pl.pallas_call(
         functools.partial(smooth_body, tiles_down, tile_rows, chips),
         out_shape=jax.ShapeDtypeStruct((devices, count * tile_rows, LANES), jnp.float32),
-        in_specs=[pl.BlockSpec(memory_space=pltpu.SMEM), pl.BlockSpec(memory_space=pltpu.HBM)]
+        in_specs=[pl.BlockSpec(memory_space=pltpu.SMEM)] * 2
+        + [pl.BlockSpec(memory_space=pltpu.HBM)]
         + [pl.BlockSpec(memory_space=pltpu.VMEM)] * 2,
         out_specs=pl.BlockSpec(memory_space=pltpu.HBM),
         scratch_shapes=[pltpu.VMEM((count, height, width), jnp.float32)]
         + [pltpu.VMEM((across, height, LANES), jnp.float32)] * 3
         + [pltpu.VMEM((across, height + 2 * SUB, LANES), jnp.float32)] * 2
         + [pltpu.VMEM((2, devices, tile_rows, LANES), jnp.float32)]
-        + [pltpu.SemaphoreType.DMA((count,)), pltpu.SemaphoreType.DMA((2,))],
+        + [pltpu.SemaphoreType.DMA((count,)), pltpu.SemaphoreType.DMA((2, 2))],
         compiler_params=pltpu.CompilerParams(vmem_limit_bytes=50 << 20),
         name="smooth",
-    )(core, frames, mine, other)
+    )(core, table, frames, mine, other)
 
 
 def convolve_body(count, rows, x_ref, high_ref, low_ref, out_ref, loaded, high, low, ready, load_sem, early_sem, late_sem):
@@ -220,26 +233,40 @@
     )(blocks.reshape(devices * count * tile_rows, LANES), high, low)
 
 
-def maps_body(class_ref, mask_ref, effusivity_ref, conductivity_ref, out_ref):
-    classes, mask = class_ref[...], mask_ref[...].astype(jnp.float32)
-    rows = classes.shape[0]
-    gain = lateral = jnp.zeros_like(mask)
-    for k in range(effusivity_ref.shape[0]):
-        gain = jnp.where(classes == k, effusivity_ref[k], gain)
-        lateral = jnp.where(classes == k, conductivity_ref[k], lateral)
-    gain, lateral = flux_factor * gain * mask, lateral_rate * lateral * mask
-    out_ref[0:rows, :] = gain
-    out_ref[rows : 2 * rows, :] = lateral
-
-
-def maps_for(class_index, surface_mask, effusivity, conductivity):
-    rows = class_index.shape[0]
+def lookup(classes, mask, entry, count):
+    result = jnp.zeros(classes.shape, jnp.float32)
+    for k in range(count):
+        result = jnp.where(classes == k, entry(k), result)
+    return jnp.where(mask != 0, result, 0.0)
+
+
+def lateral_body(class_ref, mask_ref, effusivity_ref, conductivity_ref, map_ref, table_ref, shared_ref):
+    count = conductivity_ref.shape[0]
+    rates = [lateral_rate * conductivity_ref[k] for k in range(count)]
+    shared = jnp.int32(0)
+    for k in range(count):
+        table_ref[0, k] = rates[k]
+        table_ref[1, k] = flux_factor * effusivity_ref[k]
+        for other in range(k):
+            shared = shared | (rates[k] == rates[other]).astype(jnp.int32)
+    shared_ref[0] = shared
+    lateral = lookup(class_ref[...], mask_ref[...], lambda k: rates[k], count)
+    for peer in range(map_ref.shape[0]):
+        map_ref[peer] = lateral
+
+
+def lateral_for(peers, class_index, surface_mask, effusivity, conductivity):
+    smem, vmem = pl.BlockSpec(memory_space=pltpu.SMEM), pl.BlockSpec(memory_space=pltpu.VMEM)
     return pl.pallas_call(
-        maps_body,
-        out_shape=jax.ShapeDtypeStruct((2 * rows, LANES), jnp.float32),
-        in_specs=[pl.BlockSpec(memory_space=pltpu.VMEM)] * 2 + [pl.BlockSpec(memory_space=pltpu.SMEM)] * 2,
-        out_specs=pl.BlockSpec(memory_space=pltpu.VMEM),
-        name="maps",
+        lateral_body,
+        out_shape=(
+            jax.ShapeDtypeStruct((peers, *class_index.shape), jnp.float32),
+            jax.ShapeDtypeStruct((2, conductivity.shape[0]), jnp.float32),
+            jax.ShapeDtypeStruct((1,), jnp.int32),
+        ),
+        in_specs=[vmem, vmem, smem, smem],
+        out_specs=(vmem, smem, smem),
+        name="lateral",
     )(class_index, surface_mask, effusivity, conductivity)
 
 
@@ -250,11 +277,19 @@
     devices = tiles_down * chips * 2
     core = lax.axis_index("core")
 
-    maps = maps_for(class_index, surface_mask, effusivity, conductivity)
-    for_all = jnp.broadcast_to(maps[None], (tiles_down * chips, *maps.shape))
-    mine = lax.all_to_all(for_all, ("row", "chip"), split_axis=0, concat_axis=0, tiled=True)
-    other = lax.ppermute(mine, "core", [(0, 1), (1, 0)])
-    blocks = smooth(core[None].astype(jnp.int32), frames, mine, other, tiles_down, tile_rows, chips)
+    peers = tiles_down * chips
+    lateral, table, shared = lateral_for(peers, class_index, surface_mask, effusivity, conductivity)
+
+    def smoothed(maps):
+        mine = lax.all_to_all(maps, ("row", "chip"), split_axis=0, concat_axis=0, tiled=True)
+        other = lax.ppermute(mine, "core", [(0, 1), (1, 0)])
+        return smooth(core[None].astype(jnp.int32), table, frames, mine, other, tiles_down, tile_rows, chips)
+
+    def from_both():
+        gain = lookup(class_index, surface_mask, lambda k: table[1, k], table.shape[1])
+        return smoothed(jnp.concatenate([lateral, jnp.broadcast_to(gain[None], lateral.shape)], axis=1))
+
+    blocks = lax.cond(shared[0] != 0, from_both, lambda: smoothed(lateral))
 
     frame_ids = jnp.arange(devices * count, dtype=jnp.int32)
     quarter = devices // 4

time: 110 us -> 105 us (0.955)
  blocking collectives: 27.7 us -> 22.2 us
  Pallas kernels: 17.9 us -> 19 us
    all_to_all x1, blocking collectives: 27.7 us -> 22.2 us  [smoothed(): lax.all_to_all(maps, ('row', 'chip'), split_axis=0, concat_axis=0, tiled=...]
where the time goes in v4:
time: 105 us
  waiting for transfers between devices  53.9 us (51%)
  blocking collectives  22.2 us (21%)
  Pallas kernels  19 us (18%)
  starting transfers between devices  7.28 us (7%)
  other arithmetic  1.93 us (2%)
    all_to_all x1, waiting for transfers between devices, per_device(): lax.all_to_all(blocks, ALL, split_axis=0, concat_axis=0, tiled=True)  52 us
    all_to_all x1, blocking collectives, smoothed(): lax.all_to_all(maps, ('row', 'chip'), split_axis=0, concat_axis=0, tiled=...  22.2 us
    pallas_call x1, Pallas kernels, smooth(): pl.pallas_call(functools.partial(smooth_body, tiles_down, tile_rows, chip...  10.3 us
    all_to_all x1, starting transfers between devices, per_device(): lax.all_to_all(blocks, ALL, split_axis=0, concat_axis=0, tiled=True)  7.28 us
    pallas_call x1, Pallas kernels, convolve(): pl.pallas_call(functools.partial(convolve_body, count, tile_rows), out_sh...  7.24 us
  transfers between devices with their start and end apart: 2, of which 2 were waited for; matrix products, arithmetic and copies ran while one was open for 2% of the time, Pallas kernels for 0%

profile of v4, /device:TPU:4, one launch (start us, length us, event | category | flops | bytes accessed | tf_op | source)
XLA Modules:
  0.0 105.2 jit_solution(17502851125530836799)
XLA Ops:
  0.0 1.5 %lateral.1 = (f32[64,16,128]{2,1,0:T(8,128)S(1)}, f32[2,8]{1,0:T(2,128)S(1)}, s32[1]{0:T(128)}) custom-call(s32[16,128]{1,0:T(8,128)} %class_ref.1, s32[16,128]{1,0:T(8,128)} %mask_ref.1, f32[8]{0:T(128)} %effusivity_ref.1, f32[8]{0:T(128)} %conductivity_ref.1), custom_call_target="tpu_custom_call" | custom-call | tf_op jit(solution)/shard_map/lateral/pallas_call | solution.py:260
  2.1 34.4 %conditional.1 = (f32[128,64,128]{2,1,0:T(8,128)}) conditional(s32[]{:T(128)} %bitcast.10, (s32[]{:T(128)}, f32[64,16,128]{2,1,0:T(8,128)S(1)}, f32[2,8]{1,0:T(2,128)S(1)}, f32[4,128,2048]{2,1,0:T(8,128)}) %tuple.11, (s32[]{:T(128)}, s32[16,128]{1,0:T(8,128)}, s32[16,128]{1,0:T(8,128)}, f32[2,8]{1,0:T(2,128)S(1)}, f32[64,16,128]{2,1,0:T(8,128)S(1)}, ...), branch_computations={%region_0.0_spmd, %region_1.2_spmd} | conditional | flops 299008 | bytes 25723052 | solution.py:292
  2.1 22.2 %all_to_all.13.mine_ref = f32[64,16,128]{2,1,0:T(8,128)S(1)} all-to-all(f32[64,16,128]{2,1,0:T(8,128)S(1)} %get-tuple-element.31), channel_id=1, replica_groups=mesh['row'=8,'chip'=8,'core'=2] {'row','chip'}, dimensions={0} | all-to-all | bytes 1048576 | tf_op jit(solution)/shard_map/cond/branch_0_fun/all_to_all | solution.py:284
  24.3 0.0 collective-permute-start
  24.3 1.9 %collective-permute-done.other_ref = f32[64,16,128]{2,1,0:T(8,128)S(1)} collective-permute-done((f32[64,16,128]{2,1,0:T(8,128)S(1)}, f32[64,16,128]{2,1,0:T(8,128)S(1)}, u32[]{:S(2)}, u32[]{:S(2)}) %collective-permute-start) | collective-permute-done | bytes 524320 | tf_op jit(solution)/shard_map/cond/branch_0_fun/ppermute | solution.py:285
  26.2 10.3 %smooth.2 = f32[128,64,128]{2,1,0:T(8,128)} custom-call(s32[1]{0:T(128)} %bitcast.core_ref, f32[2,8]{1,0:T(2,128)S(1)} %get-tuple-element.29.table_ref, f32[4,128,2048]{2,1,0:T(8,128)} %get-tuple-element.30.frames_ref, f32[64,16,128]{2,1,0:T(8,128)S(1)} %all_to_all.13.mine_ref, f32[64,16,128]{2,1,0:T(8,128)S(1)} %collective-permute-done.other_ref), custom_call_target="tpu_custom_call" | custom-call | tf_op jit(solution)/shard_map/cond/branch_0_fun/smooth/pallas_call | solution.py:141
  36.5 7.3 %all-to-all-start.2 = ((f32[128,64,128]{2,1,0:T(8,128)}), f32[128,64,128]{2,1,0:T(8,128)}, u32[]{:S(2)}, u32[]{:S(2)}) async-start(f32[128,64,128]{2,1,0:T(8,128)} %get-tuple-element.54), calls=%async_computation.2 | async-start | bytes 8388608 | tf_op jit(solution)/shard_map/all_to_all | solution.py:302
  43.8 1.9 %fusion = (bf16[512,512]{1,0:T(8,128)(2,1)S(1)}, bf16[512,512]{1,0:T(8,128)(2,1)S(1)}) fusion(s32[512]{0:T(512)S(1)} %fusion.9), kind=kLoop, calls=%fused_computation.4 | loop fusion | flops 5242880 | bytes 1050624 | tf_op jit(solution)/shard_map/convert_element_type | solution.py:300
  45.8 52.0 %all-to-all-done.2 = f32[128,64,128]{2,1,0:T(8,128)} async-done(((f32[128,64,128]{2,1,0:T(8,128)}), f32[128,64,128]{2,1,0:T(8,128)}, u32[]{:S(2)}, u32[]{:S(2)}) %all-to-all-start.2) | async-done | bytes 4194336 | tf_op jit(solution)/shard_map/all_to_all | solution.py:302
  97.8 7.2 %convolve.1 = f32[16,128,512]{2,1,0:T(8,128)} custom-call(f32[8192,128]{1,0:T(8,128)} %bitcast.11.x_ref, bf16[512,512]{1,0:T(8,128)(2,1)S(1)} %get-tuple-element.53.high_ref, bf16[512,512]{1,0:T(8,128)(2,1)S(1)} %get-tuple-element.52.low_ref), custom_call_target="tpu_custom_call" | custom-call | tf_op jit(solution)/shard_map/convolve/pallas_call | solution.py:221
  (1 shorter events, 0.0 us)
Async XLA Ops:
  24.3 1.9 %collective-permute-start = (f32[64,16,128]{2,1,0:T(8,128)S(1)}, f32[64,16,128]{2,1,0:T(8,128)S(1)}, u32[]{:S(2)}, u32[]{:S(2)}) collective-permute-start(f32[64,16,128]{2,1,0:T(8,128)S(1)} %all_to_all.13.mine_ref), channel_id=1, source_target_pairs={{0,1},{1,0},{2,3},{3,2},{4,5},{5,4},{6,7},{7,6},{8,9},{9,8},{10,11... | collective-permute-start | bytes 1572872 | tf_op jit(solution)/shard_map/cond/branch_0_fun/ppermute | solution.py:285
  36.5 61.2 %all-to-all-start.2 = ((f32[128,64,128]{2,1,0:T(8,128)}), f32[128,64,128]{2,1,0:T(8,128)}, u32[]{:S(2)}, u32[]{:S(2)}) async-start(f32[128,64,128]{2,1,0:T(8,128)} %get-tuple-element.54), calls=%async_computation.2 | async-start | bytes 8388608 | tf_op jit(solution)/shard_map/all_to_all | solution.py:302

commit v5 on v4

--- a/solution.py
+++ b/solution.py
@@ -28,9 +28,43 @@
     return weights(lagged) - weights(lagged - 1.0)
 
 
+def gain_of(maps, tile_rows, table_ref):
+    if maps.shape[0] == 2 * tile_rows:
+        return maps[tile_rows:]
+    found = jnp.zeros_like(maps)
+    for k in range(table_ref.shape[1]):
+        found = jnp.where(maps == table_ref[0, k], table_ref[1, k], found)
+    return found
+
+
+def prime_body(tile_rows, table_ref, frames_ref, mine_ref, frame_ref, gain_ref, sem):
+    load = pltpu.make_async_copy(frames_ref.at[0], frame_ref, sem)
+    load.start()
+    for part in range(mine_ref.shape[0]):
+        gain_ref[part] = gain_of(mine_ref[part], tile_rows, table_ref)
+    load.wait()
+
+
+def prime(table, frames, mine, tile_rows):
+    smem, vmem = pl.BlockSpec(memory_space=pltpu.SMEM), pl.BlockSpec(memory_space=pltpu.VMEM)
+    return pl.pallas_call(
+        functools.partial(prime_body, tile_rows),
+        out_shape=(
+            jax.ShapeDtypeStruct(frames.shape[1:], jnp.float32),
+            jax.ShapeDtypeStruct((mine.shape[0], tile_rows, LANES), jnp.float32),
+        ),
+        in_specs=[smem, pl.BlockSpec(memory_space=pltpu.HBM), vmem],
+        out_specs=(vmem, vmem),
+        scratch_shapes=[pltpu.SemaphoreType.DMA],
+        compiler_params=pltpu.CompilerParams(vmem_limit_bytes=50 << 20),
+        cost_estimate=pl.CostEstimate(flops=16 << 18, bytes_accessed=4 << 20, transcendentals=0),
+        name="prime",
+    )(table, frames, mine)
+
+
 def smooth_body(
     tiles_down, tile_rows, chips,
-    core_ref, table_ref, frames_ref, mine_ref, other_ref, out_ref,
+    core_ref, table_ref, frames_ref, frame_ref, gain_ref, mine_ref, other_ref, out_ref,
     loaded, gain, lat, own, ping, pong, ready, load_sem, store_sem,
 ):
     tiles_across = 2 * chips
@@ -39,30 +73,26 @@
     steps = rows // SUB
 
     def load(f):
-        return pltpu.make_async_copy(frames_ref.at[f], loaded.at[f], load_sem.at[f])
+        return pltpu.make_async_copy(frames_ref.at[f], loaded.at[f - 1], load_sem.at[f - 1])
 
     def deliver(slot, f, half):
         part = pl.ds(pl.multiple_of(f * tile_rows, tile_rows), tile_rows)
         to = pl.ds(half * (tiles_down // 2) * tiles_across, tiles_down // 2 * tiles_across)
         return pltpu.make_async_copy(ready.at[slot, to], out_ref.at[to, part, :], store_sem.at[slot, half])
 
-    load(0).start()
+    load(1).start()
     for tile in range(tiles_down):
         for chip in range(chips):
             part = tile * chips + chip
             at = pl.ds(tile * tile_rows, tile_rows)
-            for ref, index in ((mine_ref, 2 * chip + core), (other_ref, 2 * chip + 1 - core)):
-                lateral = ref[part, 0:tile_rows, :]
-                if ref.shape[1] == 2 * tile_rows:
-                    gain[index, at, :] = ref[part, tile_rows : 2 * tile_rows, :]
-                else:
-                    found = jnp.zeros_like(lateral)
-                    for k in range(table_ref.shape[1]):
-                        found = jnp.where(lateral == table_ref[0, k], table_ref[1, k], found)
-                    gain[index, at, :] = found
+            maps = other_ref[part]
+            gains = (gain_ref[part], gain_of(maps, tile_rows, table_ref))
+            for index, lateral, factor in zip(
+                (2 * chip + core, 2 * chip + 1 - core), (mine_ref[part, 0:tile_rows, :], maps[0:tile_rows]), gains
+            ):
+                gain[index, at, :] = factor
                 lat[index, at, :] = lateral
                 own[index, at, :] = 1.0 - 4.0 * lateral
-    load(1).start()
     zero = jnp.zeros((SUB, LANES), jnp.float32)
     for buffer in (ping, pong):
         for c in range(tiles_across):
@@ -104,17 +134,27 @@
 
         return store
 
+    def enter(frame):
+        for c in range(tiles_across):
+            ping[c, SUB : SUB + rows, :] = frame[:, c * LANES : (c + 1) * LANES] * gain[c]
+
+    enter(frame_ref)
+
     @pl.loop(0, count)
     def _(f):
         slot = f % 2
-        load(f).wait()
-
-        @pl.when(f + 2 < count)
+
+        @pl.when(f > 0)
         def _():
-            load(f + 2).start()
-
-        for c in range(tiles_across):
-            ping[c, SUB : SUB + rows, :] = loaded[f, :, c * LANES : (c + 1) * LANES] * gain[c]
+            load(f).wait()
+            enter(loaded.at[f - 1])
+
+        @pl.when(f + 1 < count)
+        def _():
+            @pl.when(f > 0)
+            def _():
+                load(f + 1).start()
+
         one_pass(ping, into(pong))
         one_pass(pong, into(ping))
 
@@ -134,7 +174,7 @@
             deliver(f % 2, f, half).wait()
 
 
-def smooth(core, table, frames, mine, other, tiles_down, tile_rows, chips):
+def smooth(core, table, frames, frame, gain, mine, other, tiles_down, tile_rows, chips):
     count, height, width = frames.shape
     across = 2 * chips
     devices = tiles_down * across
@@ -143,16 +183,16 @@
         out_shape=jax.ShapeDtypeStruct((devices, count * tile_rows, LANES), jnp.float32),
         in_specs=[pl.BlockSpec(memory_space=pltpu.SMEM)] * 2
         + [pl.BlockSpec(memory_space=pltpu.HBM)]
-        + [pl.BlockSpec(memory_space=pltpu.VMEM)] * 2,
+        + [pl.BlockSpec(memory_space=pltpu.VMEM)] * 4,
         out_specs=pl.BlockSpec(memory_space=pltpu.HBM),
-        scratch_shapes=[pltpu.VMEM((count, height, width), jnp.float32)]
+        scratch_shapes=[pltpu.VMEM((count - 1, height, width), jnp.float32)]
         + [pltpu.VMEM((across, height, LANES), jnp.float32)] * 3
         + [pltpu.VMEM((across, height + 2 * SUB, LANES), jnp.float32)] * 2
         + [pltpu.VMEM((2, devices, tile_rows, LANES), jnp.float32)]
-        + [pltpu.SemaphoreType.DMA((count,)), pltpu.SemaphoreType.DMA((2, 2))],
+        + [pltpu.SemaphoreType.DMA((count - 1,)), pltpu.SemaphoreType.DMA((2, 2))],
         compiler_params=pltpu.CompilerParams(vmem_limit_bytes=50 << 20),
         name="smooth",
-    )(core, table, frames, mine, other)
+    )(core, table, frames, frame, gain, mine, other)
 
 
 def convolve_body(count, rows, x_ref, high_ref, low_ref, out_ref, loaded, high, low, ready, load_sem, early_sem, late_sem):
@@ -195,19 +235,22 @@
     for k in range(groups):
         prepare(0, k)
     load(1).wait()
+    prepare(1, 0)
     for k in range(groups):
-        part = slice(k * ROW_GROUP, (k + 1) * ROW_GROUP)
-        prepare(1, k)
-        ready[part, :, first] = product(k, first, first)
+        if k + 1 < groups:
+            prepare(1, k + 1)
+        else:
+            load(2).wait()
+            load(3).wait()
+            prepare(2, 0)
+            prepare(3, 0)
+        ready[k * ROW_GROUP : (k + 1) * ROW_GROUP, :, first] = product(k, first, first)
         save(k, first, early_sem).start()
-        ready[part, :, second] = product(k, first, second)
-    load(2).wait()
-    load(3).wait()
     for k in range(groups):
-        part = slice(k * ROW_GROUP, (k + 1) * ROW_GROUP)
-        prepare(2, k)
-        prepare(3, k)
-        ready[part, :, second] = ready[part, :, second] + product(k, second, second)
+        if k + 1 < groups:
+            prepare(2, k + 1)
+            prepare(3, k + 1)
+        ready[k * ROW_GROUP : (k + 1) * ROW_GROUP, :, second] = product(k, slice(0, outputs), second)
         save(k, second, late_sem).start()
     for k in range(groups):
         save(k, first, early_sem).wait()
@@ -283,7 +326,9 @@
     def smoothed(maps):
         mine = lax.all_to_all(maps, ("row", "chip"), split_axis=0, concat_axis=0, tiled=True)
         other = lax.ppermute(mine, "core", [(0, 1), (1, 0)])
-        return smooth(core[None].astype(jnp.int32), table, frames, mine, other, tiles_down, tile_rows, chips)
+        frame, gain = prime(table, frames, mine, tile_rows)
+        number = core[None].astype(jnp.int32)
+        return smooth(number, table, frames, frame, gain, mine, other, tiles_down, tile_rows, chips)
 
     def from_both():
         gain = lookup(class_index, surface_mask, lambda k: table[1, k], table.shape[1])

time: 105 us -> 105 us (level)
  waiting for transfers between devices: 53.9 us -> 52.1 us
    ppermute x1, waiting for transfers between devices: 1.91 us -> 0.12 us  [smoothed(): other = lax.ppermute(mine, 'core', [(0, 1), (1, 0)])]
    pallas_call x0 -> x1, Pallas kernels: none -> 1.78 us  [prime(): pl.pallas_call(functools.partial(prime_body, tile_rows), out_shape=(jax.S...]
  transfers between devices with their start and end apart: 2 -> 2, of which waited for: 2 -> 2; matrix products, arithmetic and copies ran while one was open for 2% -> 2% of each run, Pallas kernels for 0% -> 2%
where the time goes in v5:
time: 105 us; the launch traced here: 104 us
  waiting for transfers between devices  52.1 us (50%)
  blocking collectives  22.5 us (21%)
  Pallas kernels  19.7 us (19%)
  starting transfers between devices  7.27 us (7%)
  other arithmetic  1.93 us (2%)
    all_to_all x1, waiting for transfers between devices, per_device(): lax.all_to_all(blocks, ALL, split_axis=0, concat_axis=0, tiled=True)  52 us
    all_to_all x1, blocking collectives, smoothed(): lax.all_to_all(maps, ('row', 'chip'), split_axis=0, concat_axis=0, tiled=...  22.5 us
    pallas_call x1, Pallas kernels, smooth(): pl.pallas_call(functools.partial(smooth_body, tiles_down, tile_rows, chip...  9.51 us
    all_to_all x1, starting transfers between devices, per_device(): lax.all_to_all(blocks, ALL, split_axis=0, concat_axis=0, tiled=True)  7.27 us
    pallas_call x1, Pallas kernels, convolve(): pl.pallas_call(functools.partial(convolve_body, count, tile_rows), out_sh...  6.94 us
  transfers between devices with their start and end apart: 2, of which 2 were waited for; matrix products, arithmetic and copies ran while one was open for 2% of the time, Pallas kernels for 2%

profile of v5, /device:TPU:4, one launch (start us, length us, event | category | flops | bytes accessed | tf_op | source)
XLA Modules:
  0.0 104.3 jit_solution(9543241972073600434)
XLA Ops:
  0.0 1.5 %lateral.1 = (f32[64,16,128]{2,1,0:T(8,128)S(1)}, f32[2,8]{1,0:T(2,128)S(1)}, s32[1]{0:T(128)}) custom-call(s32[16,128]{1,0:T(8,128)} %class_ref.1, s32[16,128]{1,0:T(8,128)} %mask_ref.1, f32[8]{0:T(128)} %effusivity_ref.1, f32[8]{0:T(128)} %conductivity_ref.1), custom_call_target="tpu_custom_call" | custom-call | tf_op jit(solution)/shard_map/lateral/pallas_call | solution.py:303
  2.1 33.9 %conditional.1 = (f32[128,64,128]{2,1,0:T(8,128)}) conditional(s32[]{:T(128)} %bitcast.10, (s32[]{:T(128)}, f32[64,16,128]{2,1,0:T(8,128)S(1)}, f32[2,8]{1,0:T(2,128)S(1)}, f32[4,128,2048]{2,1,0:T(8,128)}) %tuple.11, (s32[]{:T(128)}, s32[16,128]{1,0:T(8,128)}, s32[16,128]{1,0:T(8,128)}, f32[2,8]{1,0:T(2,128)S(1)}, f32[64,16,128]{2,1,0:T(8,128)S(1)}, ...), branch_computations={%region_0.0_spmd, %region_1.2_spmd} | conditional | flops 4493312 | bytes 29917356 | solution.py:337
  2.1 0.0 copy-start
  2.1 22.5 %all_to_all.13.mine_ref = f32[64,16,128]{2,1,0:T(8,128)S(1)} all-to-all(f32[64,16,128]{2,1,0:T(8,128)S(1)} %get-tuple-element.31), channel_id=1, replica_groups=mesh['row'=8,'chip'=8,'core'=2] {'row','chip'}, dimensions={0} | all-to-all | bytes 1048576 | tf_op jit(solution)/shard_map/cond/branch_0_fun/all_to_all | solution.py:327
  24.6 0.0 collective-permute-start
  24.6 1.8 %prime.2 = (f32[128,2048]{1,0:T(8,128)S(1)}, f32[64,16,128]{2,1,0:T(8,128)S(1)}) custom-call(f32[2,8]{1,0:T(2,128)S(1)} %get-tuple-element.29.table_ref, f32[4,128,2048]{2,1,0:T(8,128)} %get-tuple-element.30.frames_ref, f32[64,16,128]{2,1,0:T(8,128)S(1)} %all_to_all.13.mine_ref), custom_call_target="tpu_custom_call" | custom-call | flops 4194304 | bytes 4194304 | tf_op jit(solution)/shard_map/cond/branch_0_fun/prime/pallas_call | solution.py:50
  26.4 0.1 collective-permute-done.other_ref
  26.5 0.0 copy-done
  26.5 9.5 %smooth.2 = f32[128,64,128]{2,1,0:T(8,128)} custom-call(s32[1]{0:T(128)} %bitcast.core_ref, f32[2,8]{1,0:T(2,128)S(1)} %get-tuple-element.29.table_ref, f32[4,128,2048]{2,1,0:T(8,128)S(1)} %copy-done, f32[128,2048]{1,0:T(8,128)S(1)} %get-tuple-element.32.frame_ref, f32[64,16,128]{2,1,0:T(8,128)S(1)} %get-tuple-element.33.gain_ref, ...), custom_call_target="tpu_custom_call" | custom-call | tf_op jit(solution)/shard_map/cond/branch_0_fun/smooth/pallas_call | solution.py:181
  36.0 7.3 %all-to-all-start.2 = ((f32[128,64,128]{2,1,0:T(8,128)}), f32[128,64,128]{2,1,0:T(8,128)}, u32[]{:S(2)}, u32[]{:S(2)}) async-start(f32[128,64,128]{2,1,0:T(8,128)} %get-tuple-element.58), calls=%async_computation.2 | async-start | bytes 8388608 | tf_op jit(solution)/shard_map/all_to_all | solution.py:347
  43.3 1.9 %fusion = (bf16[512,512]{1,0:T(8,128)(2,1)S(1)}, bf16[512,512]{1,0:T(8,128)(2,1)S(1)}) fusion(s32[512]{0:T(512)S(1)} %fusion.9), kind=kLoop, calls=%fused_computation.4 | loop fusion | flops 5242880 | bytes 1050624 | tf_op jit(solution)/shard_map/convert_element_type | solution.py:345
  45.2 52.0 %all-to-all-done.2 = f32[128,64,128]{2,1,0:T(8,128)} async-done(((f32[128,64,128]{2,1,0:T(8,128)}), f32[128,64,128]{2,1,0:T(8,128)}, u32[]{:S(2)}, u32[]{:S(2)}) %all-to-all-start.2) | async-done | bytes 4194336 | tf_op jit(solution)/shard_map/all_to_all | solution.py:347
  97.2 6.9 %convolve.1 = f32[16,128,512]{2,1,0:T(8,128)} custom-call(f32[8192,128]{1,0:T(8,128)} %bitcast.11.x_ref, bf16[512,512]{1,0:T(8,128)(2,1)S(1)} %get-tuple-element.57.high_ref, bf16[512,512]{1,0:T(8,128)(2,1)S(1)} %get-tuple-element.56.low_ref), custom_call_target="tpu_custom_call" | custom-call | tf_op jit(solution)/shard_map/convolve/pallas_call | solution.py:264
  (1 shorter events, 0.0 us)
Async XLA Ops:
  2.1 24.4 %copy-start = (f32[4,128,2048]{2,1,0:T(8,128)S(1)}, f32[4,128,2048]{2,1,0:T(8,128)}, u32[]{:S(2)}) copy-start(f32[4,128,2048]{2,1,0:T(8,128)} %get-tuple-element.30.frames_ref) | copy-start | bytes 12582916 | tf_op jit(solution)/shard_map/cond
  24.6 1.9 %collective-permute-start = (f32[64,16,128]{2,1,0:T(8,128)S(1)}, f32[64,16,128]{2,1,0:T(8,128)S(1)}, u32[]{:S(2)}, u32[]{:S(2)}) collective-permute-start(f32[64,16,128]{2,1,0:T(8,128)S(1)} %all_to_all.13.mine_ref), channel_id=1, source_target_pairs={{0,1},{1,0},{2,3},{3,2},{4,5},{5,4},{6,7},{7,6},{8,9},{9,8},{10,11... | collective-permute-start | bytes 1572872 | tf_op jit(solution)/shard_map/cond/branch_0_fun/ppermute | solution.py:328
  36.0 61.2 %all-to-all-start.2 = ((f32[128,64,128]{2,1,0:T(8,128)}), f32[128,64,128]{2,1,0:T(8,128)}, u32[]{:S(2)}, u32[]{:S(2)}) async-start(f32[128,64,128]{2,1,0:T(8,128)} %get-tuple-element.58), calls=%async_computation.2 | async-start | bytes 8388608 | tf_op jit(solution)/shard_map/all_to_all | solution.py:347

commit v6 on v5

--- a/solution.py
+++ b/solution.py
@@ -196,24 +196,24 @@
 
 
 def convolve_body(count, rows, x_ref, high_ref, low_ref, out_ref, loaded, high, low, ready, load_sem, early_sem, late_sem):
-    quarters, chunk, _ = loaded.shape
-    sources = chunk // (count * rows)
+    quarters, sources, pitch, _ = loaded.shape
     outputs = out_ref.shape[2]
     half = outputs // 2
     first, second = slice(0, half), slice(half, outputs)
     groups = rows // ROW_GROUP
 
     def load(q):
-        return pltpu.make_async_copy(x_ref.at[pl.ds(q * chunk, chunk)], loaded.at[q], load_sem.at[q])
+        part = pl.ds(q * sources, sources)
+        return pltpu.make_async_copy(x_ref.at[part], loaded.at[q, :, 0 : count * rows, :], load_sem.at[q])
 
     def save(k, columns, sem):
         part = slice(k * ROW_GROUP, (k + 1) * ROW_GROUP)
         return pltpu.make_async_copy(ready.at[part, :, columns], out_ref.at[part, :, columns], sem.at[k])
 
     def prepare(q, k):
-        flat = loaded.at[q]
+        flat = loaded.at[q].reshape(sources * pitch, LANES)
         for r in range(k * ROW_GROUP, (k + 1) * ROW_GROUP):
-            parts = [flat[pl.ds(f * rows + r, sources, stride=count * rows), :] for f in range(count)]
+            parts = [flat[pl.ds(f * rows + r, sources, stride=pitch), :] for f in range(count)]
             x = jnp.concatenate(parts, axis=0).T
             top = x.astype(jnp.bfloat16)
             at = (slice(r * LANES, (r + 1) * LANES), slice(q * LANES, (q + 1) * LANES))
@@ -266,14 +266,14 @@
         out_shape=jax.ShapeDtypeStruct((tile_rows, LANES, frames), jnp.float32),
         in_specs=[pl.BlockSpec(memory_space=pltpu.HBM)] + [pl.BlockSpec(memory_space=pltpu.VMEM)] * 2,
         out_specs=pl.BlockSpec(memory_space=pltpu.HBM),
-        scratch_shapes=[pltpu.VMEM((quarters, devices // quarters * count * tile_rows, LANES), jnp.float32)]
+        scratch_shapes=[pltpu.VMEM((quarters, devices // quarters, count * tile_rows + SUB, LANES), jnp.float32)]
         + [pltpu.VMEM((tile_rows * LANES, frames), jnp.bfloat16)] * 2
         + [pltpu.VMEM((tile_rows, LANES, frames), jnp.float32)]
         + [pltpu.SemaphoreType.DMA((quarters,))]
         + [pltpu.SemaphoreType.DMA((tile_rows // ROW_GROUP,))] * 2,
         compiler_params=pltpu.CompilerParams(vmem_limit_bytes=50 << 20),
         name="convolve",
-    )(blocks.reshape(devices * count * tile_rows, LANES), high, low)
+    )(blocks, high, low)
 
 
 def lookup(classes, mask, entry, count):

time: 105 us -> 103 us (0.981)
  Pallas kernels: 19.7 us -> 18.3 us
    pallas_call x1, Pallas kernels: 6.94 us -> 5.55 us  [convolve(): pl.pallas_call(functools.partial(convolve_body, count, tile_rows), out_sh...]
where the time goes in v6:
time: 103 us
  waiting for transfers between devices  52.1 us (51%)
  blocking collectives  22.5 us (22%)
  Pallas kernels  18.3 us (18%)
  starting transfers between devices  7.27 us (7%)
  other arithmetic  1.93 us (2%)
    all_to_all x1, waiting for transfers between devices, per_device(): lax.all_to_all(blocks, ALL, split_axis=0, concat_axis=0, tiled=True)  52 us
    all_to_all x1, blocking collectives, smoothed(): lax.all_to_all(maps, ('row', 'chip'), split_axis=0, concat_axis=0, tiled=...  22.5 us
    pallas_call x1, Pallas kernels, smooth(): pl.pallas_call(functools.partial(smooth_body, tiles_down, tile_rows, chip...  9.51 us
    all_to_all x1, starting transfers between devices, per_device(): lax.all_to_all(blocks, ALL, split_axis=0, concat_axis=0, tiled=True)  7.27 us
    pallas_call x1, Pallas kernels, convolve(): pl.pallas_call(functools.partial(convolve_body, count, tile_rows), out_sh...  5.55 us
  transfers between devices with their start and end apart: 2, of which 2 were waited for; matrix products, arithmetic and copies ran while one was open for 2% of the time, Pallas kernels for 2%

profile of v6, /device:TPU:4, one launch (start us, length us, event | category | flops | bytes accessed | tf_op | source)
XLA Modules:
  0.0 103.0 jit_solution(6722496697105134156)
XLA Ops:
  0.0 1.5 %lateral.1 = (f32[64,16,128]{2,1,0:T(8,128)S(1)}, f32[2,8]{1,0:T(2,128)S(1)}, s32[1]{0:T(128)}) custom-call(s32[16,128]{1,0:T(8,128)} %class_ref.1, s32[16,128]{1,0:T(8,128)} %mask_ref.1, f32[8]{0:T(128)} %effusivity_ref.1, f32[8]{0:T(128)} %conductivity_ref.1), custom_call_target="tpu_custom_call" | custom-call | tf_op jit(solution)/shard_map/lateral/pallas_call | solution.py:303
  2.1 33.9 %conditional.1 = (f32[128,64,128]{2,1,0:T(8,128)}) conditional(s32[]{:T(128)} %bitcast.10, (s32[]{:T(128)}, f32[64,16,128]{2,1,0:T(8,128)S(1)}, f32[2,8]{1,0:T(2,128)S(1)}, f32[4,128,2048]{2,1,0:T(8,128)}) %tuple.11, (s32[]{:T(128)}, s32[16,128]{1,0:T(8,128)}, s32[16,128]{1,0:T(8,128)}, f32[2,8]{1,0:T(2,128)S(1)}, f32[64,16,128]{2,1,0:T(8,128)S(1)}, ...), branch_computations={%region_0.0_spmd, %region_1.2_spmd} | conditional | flops 4493312 | bytes 29917356 | solution.py:337
  2.1 0.0 copy-start
  2.1 22.5 %all_to_all.13.mine_ref = f32[64,16,128]{2,1,0:T(8,128)S(1)} all-to-all(f32[64,16,128]{2,1,0:T(8,128)S(1)} %get-tuple-element.31), channel_id=1, replica_groups=mesh['row'=8,'chip'=8,'core'=2] {'row','chip'}, dimensions={0} | all-to-all | bytes 1048576 | tf_op jit(solution)/shard_map/cond/branch_0_fun/all_to_all | solution.py:327
  24.6 0.0 collective-permute-start
  24.6 1.8 %prime.2 = (f32[128,2048]{1,0:T(8,128)S(1)}, f32[64,16,128]{2,1,0:T(8,128)S(1)}) custom-call(f32[2,8]{1,0:T(2,128)S(1)} %get-tuple-element.29.table_ref, f32[4,128,2048]{2,1,0:T(8,128)} %get-tuple-element.30.frames_ref, f32[64,16,128]{2,1,0:T(8,128)S(1)} %all_to_all.13.mine_ref), custom_call_target="tpu_custom_call" | custom-call | flops 4194304 | bytes 4194304 | tf_op jit(solution)/shard_map/cond/branch_0_fun/prime/pallas_call | solution.py:50
  26.4 0.1 collective-permute-done.other_ref
  26.5 0.0 copy-done
  26.5 9.5 %smooth.2 = f32[128,64,128]{2,1,0:T(8,128)} custom-call(s32[1]{0:T(128)} %bitcast.core_ref, f32[2,8]{1,0:T(2,128)S(1)} %get-tuple-element.29.table_ref, f32[4,128,2048]{2,1,0:T(8,128)S(1)} %copy-done, f32[128,2048]{1,0:T(8,128)S(1)} %get-tuple-element.32.frame_ref, f32[64,16,128]{2,1,0:T(8,128)S(1)} %get-tuple-element.33.gain_ref, ...), custom_call_target="tpu_custom_call" | custom-call | tf_op jit(solution)/shard_map/cond/branch_0_fun/smooth/pallas_call | solution.py:181
  36.0 7.3 %all-to-all-start.2 = ((f32[128,64,128]{2,1,0:T(8,128)}), f32[128,64,128]{2,1,0:T(8,128)}, u32[]{:S(2)}, u32[]{:S(2)}) async-start(f32[128,64,128]{2,1,0:T(8,128)} %get-tuple-element.58), calls=%async_computation.2 | async-start | bytes 8388608 | tf_op jit(solution)/shard_map/all_to_all | solution.py:347
  43.3 1.9 %fusion = (bf16[512,512]{1,0:T(8,128)(2,1)S(1)}, bf16[512,512]{1,0:T(8,128)(2,1)S(1)}) fusion(s32[512]{0:T(512)S(1)} %fusion.9), kind=kLoop, calls=%fused_computation.4 | loop fusion | flops 5242880 | bytes 1050624 | tf_op jit(solution)/shard_map/convert_element_type | solution.py:345
  45.2 52.0 %all-to-all-done.2.x_ref = f32[128,64,128]{2,1,0:T(8,128)} async-done(((f32[128,64,128]{2,1,0:T(8,128)}), f32[128,64,128]{2,1,0:T(8,128)}, u32[]{:S(2)}, u32[]{:S(2)}) %all-to-all-start.2) | async-done | bytes 4194336 | tf_op jit(solution)/shard_map/all_to_all | solution.py:347
  97.2 5.5 %convolve.1 = f32[16,128,512]{2,1,0:T(8,128)} custom-call(f32[128,64,128]{2,1,0:T(8,128)} %all-to-all-done.2.x_ref, bf16[512,512]{1,0:T(8,128)(2,1)S(1)} %get-tuple-element.57.high_ref, bf16[512,512]{1,0:T(8,128)(2,1)S(1)} %get-tuple-element.56.low_ref), custom_call_target="tpu_custom_call" | custom-call | tf_op jit(solution)/shard_map/convolve/pallas_call | solution.py:264
  (1 shorter events, 0.0 us)
Async XLA Ops:
  2.1 24.4 %copy-start = (f32[4,128,2048]{2,1,0:T(8,128)S(1)}, f32[4,128,2048]{2,1,0:T(8,128)}, u32[]{:S(2)}) copy-start(f32[4,128,2048]{2,1,0:T(8,128)} %get-tuple-element.30.frames_ref) | copy-start | bytes 12582916 | tf_op jit(solution)/shard_map/cond
  24.6 1.9 %collective-permute-start = (f32[64,16,128]{2,1,0:T(8,128)S(1)}, f32[64,16,128]{2,1,0:T(8,128)S(1)}, u32[]{:S(2)}, u32[]{:S(2)}) collective-permute-start(f32[64,16,128]{2,1,0:T(8,128)S(1)} %all_to_all.13.mine_ref), channel_id=1, source_target_pairs={{0,1},{1,0},{2,3},{3,2},{4,5},{5,4},{6,7},{7,6},{8,9},{9,8},{10,11... | collective-permute-start | bytes 1572872 | tf_op jit(solution)/shard_map/cond/branch_0_fun/ppermute | solution.py:328
  36.0 61.2 %all-to-all-start.2 = ((f32[128,64,128]{2,1,0:T(8,128)}), f32[128,64,128]{2,1,0:T(8,128)}, u32[]{:S(2)}, u32[]{:S(2)}) async-start(f32[128,64,128]{2,1,0:T(8,128)} %get-tuple-element.58), calls=%async_computation.2 | async-start | bytes 8388608 | tf_op jit(solution)/shard_map/all_to_all | solution.py:347

commit v7 on v6

--- a/solution.py
+++ b/solution.py
@@ -11,6 +11,7 @@
 LANES = 128
 SUB = 8
 ROW_GROUP = 2
+PRODUCT_EVERY = 4
 
 flux_factor = 1.1283791670955126
 lateral_rate = 0.24
@@ -101,17 +102,32 @@
 
     lane = lax.broadcasted_iota(jnp.int32, (SUB, LANES), 1)
     first, last = lane == 0, lane == LANES - 1
+    source_lane = lax.broadcasted_iota(jnp.int32, (2 * LANES, 2 * LANES), 0) % LANES
+    target_lane = lax.broadcasted_iota(jnp.int32, (2 * LANES, 2 * LANES), 1)
+    wanted = jnp.where(target_lane < LANES, target_lane + LANES - 1, target_lane + 1) % LANES
+    both_moves = (source_lane == wanted).astype(jnp.float32).astype(jnp.bfloat16)
 
     def one_pass(source, store, after=None):
         for half in range(0, steps, SUB):
             center, right_moved, left_moved = {}, {}, {}
 
             def prepare(c):
+                by_product = c % PRODUCT_EVERY == 0
+                if by_product:
+                    block = source[c, SUB + half * SUB : SUB + (half + SUB) * SUB, :]
+                    top = block.astype(jnp.bfloat16)
+                    rest = (block - top.astype(jnp.float32)).astype(jnp.bfloat16)
+                    terms = jnp.concatenate([top, rest], axis=1)
+                    moved = jnp.dot(terms, both_moves, preferred_element_type=jnp.float32)
                 for i in range(half, half + SUB):
                     value = source[c, SUB + i * SUB : 2 * SUB + i * SUB, :]
                     center[c, i] = value
-                    right_moved[c, i] = pltpu.roll(value, 1, 1)
-                    left_moved[c, i] = pltpu.roll(value, LANES - 1, 1)
+                    if by_product:
+                        at = slice((i - half) * SUB, (i - half + 1) * SUB)
+                        right_moved[c, i], left_moved[c, i] = moved[at, :LANES], moved[at, LANES:]
+                    else:
+                        right_moved[c, i] = pltpu.roll(value, 1, 1)
+                        left_moved[c, i] = pltpu.roll(value, LANES - 1, 1)
 
             prepare(0)
             for c in range(tiles_across):

time: 103 us -> 103 us (level)
  no operation moved by 1% of the time
where the time goes in v7:
time: 103 us; the launch traced here: 102 us
  waiting for transfers between devices  52.1 us (51%)
  blocking collectives  22.5 us (22%)
  Pallas kernels  17.7 us (17%)
  starting transfers between devices  7.27 us (7%)
  other arithmetic  1.93 us (2%)
    all_to_all x1, waiting for transfers between devices, per_device(): lax.all_to_all(blocks, ALL, split_axis=0, concat_axis=0, tiled=True)  52 us
    all_to_all x1, blocking collectives, smoothed(): lax.all_to_all(maps, ('row', 'chip'), split_axis=0, concat_axis=0, tiled=...  22.5 us
    pallas_call x1, Pallas kernels, smooth(): pl.pallas_call(functools.partial(smooth_body, tiles_down, tile_rows, chip...  8.93 us
    all_to_all x1, starting transfers between devices, per_device(): lax.all_to_all(blocks, ALL, split_axis=0, concat_axis=0, tiled=True)  7.27 us
    pallas_call x1, Pallas kernels, convolve(): pl.pallas_call(functools.partial(convolve_body, count, tile_rows), out_sh...  5.54 us
  transfers between devices with their start and end apart: 2, of which 2 were waited for; matrix products, arithmetic and copies ran while one was open for 2% of the time, Pallas kernels for 2%

profile of v7, /device:TPU:4, one launch (start us, length us, event | category | flops | bytes accessed | tf_op | source)
XLA Modules:
  0.0 102.4 jit_solution(12334073064717674287)
XLA Ops:
  0.0 1.5 %lateral.1 = (f32[64,16,128]{2,1,0:T(8,128)S(1)}, f32[2,8]{1,0:T(2,128)S(1)}, s32[1]{0:T(128)}) custom-call(s32[16,128]{1,0:T(8,128)} %class_ref.1, s32[16,128]{1,0:T(8,128)} %mask_ref.1, f32[8]{0:T(128)} %effusivity_ref.1, f32[8]{0:T(128)} %conductivity_ref.1), custom_call_target="tpu_custom_call" | custom-call | tf_op jit(solution)/shard_map/lateral/pallas_call | solution.py:319
  2.1 33.3 %conditional.1 = (f32[128,64,128]{2,1,0:T(8,128)}) conditional(s32[]{:T(128)} %bitcast.10, (s32[]{:T(128)}, f32[64,16,128]{2,1,0:T(8,128)S(1)}, f32[2,8]{1,0:T(2,128)S(1)}, f32[4,128,2048]{2,1,0:T(8,128)}) %tuple.11, (s32[]{:T(128)}, s32[16,128]{1,0:T(8,128)}, s32[16,128]{1,0:T(8,128)}, f32[2,8]{1,0:T(2,128)S(1)}, f32[64,16,128]{2,1,0:T(8,128)S(1)}, ...), branch_computations={%region_0.0_spmd, %region_1.2_spmd} | conditional | flops 4493312 | bytes 29917356 | solution.py:353
  2.1 0.0 copy-start
  2.1 22.5 %all_to_all.13.mine_ref = f32[64,16,128]{2,1,0:T(8,128)S(1)} all-to-all(f32[64,16,128]{2,1,0:T(8,128)S(1)} %get-tuple-element.31), channel_id=1, replica_groups=mesh['row'=8,'chip'=8,'core'=2] {'row','chip'}, dimensions={0} | all-to-all | bytes 1048576 | tf_op jit(solution)/shard_map/cond/branch_0_fun/all_to_all | solution.py:343
  24.6 0.0 collective-permute-start
  24.6 1.8 %prime.2 = (f32[128,2048]{1,0:T(8,128)S(1)}, f32[64,16,128]{2,1,0:T(8,128)S(1)}) custom-call(f32[2,8]{1,0:T(2,128)S(1)} %get-tuple-element.29.table_ref, f32[4,128,2048]{2,1,0:T(8,128)} %get-tuple-element.30.frames_ref, f32[64,16,128]{2,1,0:T(8,128)S(1)} %all_to_all.13.mine_ref), custom_call_target="tpu_custom_call" | custom-call | flops 4194304 | bytes 4194304 | tf_op jit(solution)/shard_map/cond/branch_0_fun/prime/pallas_call | solution.py:51
  26.4 0.1 collective-permute-done.other_ref
  26.5 0.0 copy-done
  26.5 8.9 %smooth.2 = f32[128,64,128]{2,1,0:T(8,128)} custom-call(s32[1]{0:T(128)} %bitcast.core_ref, f32[2,8]{1,0:T(2,128)S(1)} %get-tuple-element.29.table_ref, f32[4,128,2048]{2,1,0:T(8,128)S(1)} %copy-done, f32[128,2048]{1,0:T(8,128)S(1)} %get-tuple-element.32.frame_ref, f32[64,16,128]{2,1,0:T(8,128)S(1)} %get-tuple-element.33.gain_ref, ...), custom_call_target="tpu_custom_call" | custom-call | tf_op jit(solution)/shard_map/cond/branch_0_fun/smooth/pallas_call | solution.py:197
  35.5 7.3 %all-to-all-start.2 = ((f32[128,64,128]{2,1,0:T(8,128)}), f32[128,64,128]{2,1,0:T(8,128)}, u32[]{:S(2)}, u32[]{:S(2)}) async-start(f32[128,64,128]{2,1,0:T(8,128)} %get-tuple-element.58), calls=%async_computation.2 | async-start | bytes 8388608 | tf_op jit(solution)/shard_map/all_to_all | solution.py:363
  42.7 1.9 %fusion = (bf16[512,512]{1,0:T(8,128)(2,1)S(1)}, bf16[512,512]{1,0:T(8,128)(2,1)S(1)}) fusion(s32[512]{0:T(512)S(1)} %fusion.9), kind=kLoop, calls=%fused_computation.4 | loop fusion | flops 5242880 | bytes 1050624 | tf_op jit(solution)/shard_map/convert_element_type | solution.py:361
  44.7 52.0 %all-to-all-done.2.x_ref = f32[128,64,128]{2,1,0:T(8,128)} async-done(((f32[128,64,128]{2,1,0:T(8,128)}), f32[128,64,128]{2,1,0:T(8,128)}, u32[]{:S(2)}, u32[]{:S(2)}) %all-to-all-start.2) | async-done | bytes 4194336 | tf_op jit(solution)/shard_map/all_to_all | solution.py:363
  96.7 5.5 %convolve.1 = f32[16,128,512]{2,1,0:T(8,128)} custom-call(f32[128,64,128]{2,1,0:T(8,128)} %all-to-all-done.2.x_ref, bf16[512,512]{1,0:T(8,128)(2,1)S(1)} %get-tuple-element.57.high_ref, bf16[512,512]{1,0:T(8,128)(2,1)S(1)} %get-tuple-element.56.low_ref), custom_call_target="tpu_custom_call" | custom-call | tf_op jit(solution)/shard_map/convolve/pallas_call | solution.py:280
  (1 shorter events, 0.0 us)
Async XLA Ops:
  2.1 24.4 %copy-start = (f32[4,128,2048]{2,1,0:T(8,128)S(1)}, f32[4,128,2048]{2,1,0:T(8,128)}, u32[]{:S(2)}) copy-start(f32[4,128,2048]{2,1,0:T(8,128)} %get-tuple-element.30.frames_ref) | copy-start | bytes 12582916 | tf_op jit(solution)/shard_map/cond
  24.6 1.9 %collective-permute-start = (f32[64,16,128]{2,1,0:T(8,128)S(1)}, f32[64,16,128]{2,1,0:T(8,128)S(1)}, u32[]{:S(2)}, u32[]{:S(2)}) collective-permute-start(f32[64,16,128]{2,1,0:T(8,128)S(1)} %all_to_all.13.mine_ref), channel_id=1, source_target_pairs={{0,1},{1,0},{2,3},{3,2},{4,5},{5,4},{6,7},{7,6},{8,9},{9,8},{10,11... | collective-permute-start | bytes 1572872 | tf_op jit(solution)/shard_map/cond/branch_0_fun/ppermute | solution.py:344
  35.5 61.2 %all-to-all-start.2 = ((f32[128,64,128]{2,1,0:T(8,128)}), f32[128,64,128]{2,1,0:T(8,128)}, u32[]{:S(2)}, u32[]{:S(2)}) async-start(f32[128,64,128]{2,1,0:T(8,128)} %get-tuple-element.58), calls=%async_computation.2 | async-start | bytes 8388608 | tf_op jit(solution)/shard_map/all_to_all | solution.py:363

commit v8 on v7

--- a/solution.py
+++ b/solution.py
@@ -79,7 +79,7 @@
     def deliver(slot, f, half):
         part = pl.ds(pl.multiple_of(f * tile_rows, tile_rows), tile_rows)
         to = pl.ds(half * (tiles_down // 2) * tiles_across, tiles_down // 2 * tiles_across)
-        return pltpu.make_async_copy(ready.at[slot, to], out_ref.at[to, part, :], store_sem.at[slot, half])
+        return pltpu.make_async_copy(ready.at[slot, to, 0:tile_rows, :], out_ref.at[to, part, :], store_sem.at[slot, half])
 
     load(1).start()
     for tile in range(tiles_down):
@@ -130,9 +130,10 @@
                         left_moved[c, i] = pltpu.roll(value, LANES - 1, 1)
 
             prepare(0)
+            prepare(1)
             for c in range(tiles_across):
-                if c + 1 < tiles_across:
-                    prepare(c + 1)
+                if c + 2 < tiles_across:
+                    prepare(c + 2)
                 for i in range(half, half + SUB):
                     at = slice(i * SUB, i * SUB + SUB)
                     up = source[c, SUB - 1 + i * SUB : 2 * SUB - 1 + i * SUB, :]
@@ -204,7 +205,7 @@
         scratch_shapes=[pltpu.VMEM((count - 1, height, width), jnp.float32)]
         + [pltpu.VMEM((across, height, LANES), jnp.float32)] * 3
         + [pltpu.VMEM((across, height + 2 * SUB, LANES), jnp.float32)] * 2
-        + [pltpu.VMEM((2, devices, tile_rows, LANES), jnp.float32)]
+        + [pltpu.VMEM((2, devices, tile_rows + SUB, LANES), jnp.float32)]
         + [pltpu.SemaphoreType.DMA((count - 1,)), pltpu.SemaphoreType.DMA((2, 2))],
         compiler_params=pltpu.CompilerParams(vmem_limit_bytes=50 << 20),
         name="smooth",
@@ -350,7 +351,7 @@
         gain = lookup(class_index, surface_mask, lambda k: table[1, k], table.shape[1])
         return smoothed(jnp.concatenate([lateral, jnp.broadcast_to(gain[None], lateral.shape)], axis=1))
 
-    blocks = lax.cond(shared[0] != 0, from_both, lambda: smoothed(lateral))
+    blocks = lax.switch(shared[0], (lambda: smoothed(lateral), from_both))
 
     frame_ids = jnp.arange(devices * count, dtype=jnp.int32)
     quarter = devices // 4

time: 103 us -> 103 us (level)
  no operation moved by 1% of the time
where the time goes in v8:
time: 103 us; the launch traced here: 102 us
  waiting for transfers between devices  52.1 us (51%)
  blocking collectives  22.5 us (22%)
  Pallas kernels  17.7 us (17%)
  starting transfers between devices  7.27 us (7%)
  other arithmetic  1.93 us (2%)
    all_to_all x1, waiting for transfers between devices, per_device(): lax.all_to_all(blocks, ALL, split_axis=0, concat_axis=0, tiled=True)  52 us
    all_to_all x1, blocking collectives, smoothed(): lax.all_to_all(maps, ('row', 'chip'), split_axis=0, concat_axis=0, tiled=...  22.5 us
    pallas_call x1, Pallas kernels, smooth(): pl.pallas_call(functools.partial(smooth_body, tiles_down, tile_rows, chip...  8.93 us
    all_to_all x1, starting transfers between devices, per_device(): lax.all_to_all(blocks, ALL, split_axis=0, concat_axis=0, tiled=True)  7.27 us
    pallas_call x1, Pallas kernels, convolve(): pl.pallas_call(functools.partial(convolve_body, count, tile_rows), out_sh...  5.54 us
  transfers between devices with their start and end apart: 2, of which 2 were waited for; matrix products, arithmetic and copies ran while one was open for 2% of the time, Pallas kernels for 2%

profile of v8, /device:TPU:4, one launch (start us, length us, event | category | flops | bytes accessed | tf_op | source)
XLA Modules:
  0.0 102.4 jit_solution(15608268266730187969)
XLA Ops:
  0.0 1.5 %lateral.1 = (f32[64,16,128]{2,1,0:T(8,128)S(1)}, f32[2,8]{1,0:T(2,128)S(1)}, s32[1]{0:T(128)}) custom-call(s32[16,128]{1,0:T(8,128)} %class_ref.1, s32[16,128]{1,0:T(8,128)} %mask_ref.1, f32[8]{0:T(128)} %effusivity_ref.1, f32[8]{0:T(128)} %conductivity_ref.1), custom_call_target="tpu_custom_call" | custom-call | tf_op jit(solution)/shard_map/lateral/pallas_call | solution.py:320
  2.1 33.3 %conditional.1 = (f32[128,64,128]{2,1,0:T(8,128)}) conditional(s32[]{:T(128)} %bitcast.10, (s32[]{:T(128)}, f32[64,16,128]{2,1,0:T(8,128)S(1)}, f32[2,8]{1,0:T(2,128)S(1)}, f32[4,128,2048]{2,1,0:T(8,128)}) %tuple.11, (s32[]{:T(128)}, s32[16,128]{1,0:T(8,128)}, s32[16,128]{1,0:T(8,128)}, f32[2,8]{1,0:T(2,128)S(1)}, f32[64,16,128]{2,1,0:T(8,128)S(1)}, ...), branch_computations={%region_0.0_spmd, %region_1.2_spmd} | conditional | flops 4493312 | bytes 29917356 | solution.py:354
  2.1 0.0 copy-start
  2.1 22.5 %all_to_all.13.mine_ref = f32[64,16,128]{2,1,0:T(8,128)S(1)} all-to-all(f32[64,16,128]{2,1,0:T(8,128)S(1)} %get-tuple-element.31), channel_id=1, replica_groups=mesh['row'=8,'chip'=8,'core'=2] {'row','chip'}, dimensions={0} | all-to-all | bytes 1048576 | tf_op jit(solution)/shard_map/cond/branch_0_fun/all_to_all | solution.py:344
  24.6 0.0 collective-permute-start
  24.6 1.8 %prime.2 = (f32[128,2048]{1,0:T(8,128)S(1)}, f32[64,16,128]{2,1,0:T(8,128)S(1)}) custom-call(f32[2,8]{1,0:T(2,128)S(1)} %get-tuple-element.29.table_ref, f32[4,128,2048]{2,1,0:T(8,128)} %get-tuple-element.30.frames_ref, f32[64,16,128]{2,1,0:T(8,128)S(1)} %all_to_all.13.mine_ref), custom_call_target="tpu_custom_call" | custom-call | flops 4194304 | bytes 4194304 | tf_op jit(solution)/shard_map/cond/branch_0_fun/prime/pallas_call | solution.py:51
  26.4 0.1 collective-permute-done.other_ref
  26.5 0.0 copy-done
  26.5 8.9 %smooth.2 = f32[128,64,128]{2,1,0:T(8,128)} custom-call(s32[1]{0:T(128)} %bitcast.core_ref, f32[2,8]{1,0:T(2,128)S(1)} %get-tuple-element.29.table_ref, f32[4,128,2048]{2,1,0:T(8,128)S(1)} %copy-done, f32[128,2048]{1,0:T(8,128)S(1)} %get-tuple-element.32.frame_ref, f32[64,16,128]{2,1,0:T(8,128)S(1)} %get-tuple-element.33.gain_ref, ...), custom_call_target="tpu_custom_call" | custom-call | tf_op jit(solution)/shard_map/cond/branch_0_fun/smooth/pallas_call | solution.py:198
  35.5 7.3 %all-to-all-start.2 = ((f32[128,64,128]{2,1,0:T(8,128)}), f32[128,64,128]{2,1,0:T(8,128)}, u32[]{:S(2)}, u32[]{:S(2)}) async-start(f32[128,64,128]{2,1,0:T(8,128)} %get-tuple-element.58), calls=%async_computation.2 | async-start | bytes 8388608 | tf_op jit(solution)/shard_map/all_to_all | solution.py:364
  42.7 1.9 %fusion = (bf16[512,512]{1,0:T(8,128)(2,1)S(1)}, bf16[512,512]{1,0:T(8,128)(2,1)S(1)}) fusion(s32[512]{0:T(512)S(1)} %fusion.9), kind=kLoop, calls=%fused_computation.4 | loop fusion | flops 5242880 | bytes 1050624 | tf_op jit(solution)/shard_map/convert_element_type | solution.py:362
  44.7 52.0 %all-to-all-done.2.x_ref = f32[128,64,128]{2,1,0:T(8,128)} async-done(((f32[128,64,128]{2,1,0:T(8,128)}), f32[128,64,128]{2,1,0:T(8,128)}, u32[]{:S(2)}, u32[]{:S(2)}) %all-to-all-start.2) | async-done | bytes 4194336 | tf_op jit(solution)/shard_map/all_to_all | solution.py:364
  96.7 5.5 %convolve.1 = f32[16,128,512]{2,1,0:T(8,128)} custom-call(f32[128,64,128]{2,1,0:T(8,128)} %all-to-all-done.2.x_ref, bf16[512,512]{1,0:T(8,128)(2,1)S(1)} %get-tuple-element.57.high_ref, bf16[512,512]{1,0:T(8,128)(2,1)S(1)} %get-tuple-element.56.low_ref), custom_call_target="tpu_custom_call" | custom-call | tf_op jit(solution)/shard_map/convolve/pallas_call | solution.py:281
  (1 shorter events, 0.0 us)
Async XLA Ops:
  2.1 24.4 %copy-start = (f32[4,128,2048]{2,1,0:T(8,128)S(1)}, f32[4,128,2048]{2,1,0:T(8,128)}, u32[]{:S(2)}) copy-start(f32[4,128,2048]{2,1,0:T(8,128)} %get-tuple-element.30.frames_ref) | copy-start | bytes 12582916 | tf_op jit(solution)/shard_map/cond
  24.6 1.9 %collective-permute-start = (f32[64,16,128]{2,1,0:T(8,128)S(1)}, f32[64,16,128]{2,1,0:T(8,128)S(1)}, u32[]{:S(2)}, u32[]{:S(2)}) collective-permute-start(f32[64,16,128]{2,1,0:T(8,128)S(1)} %all_to_all.13.mine_ref), channel_id=1, source_target_pairs={{0,1},{1,0},{2,3},{3,2},{4,5},{5,4},{6,7},{7,6},{8,9},{9,8},{10,11... | collective-permute-start | bytes 1572872 | tf_op jit(solution)/shard_map/cond/branch_0_fun/ppermute | solution.py:345
  35.5 61.2 %all-to-all-start.2 = ((f32[128,64,128]{2,1,0:T(8,128)}), f32[128,64,128]{2,1,0:T(8,128)}, u32[]{:S(2)}, u32[]{:S(2)}) async-start(f32[128,64,128]{2,1,0:T(8,128)} %get-tuple-element.58), calls=%async_computation.2 | async-start | bytes 8388608 | tf_op jit(solution)/shard_map/all_to_all | solution.py:364
